TPU v7x, 512 devices: a whole 4x8x8 slice. The times are simulated.
512 devices in a mesh: view: 4 (over x), strip: 128 (over y, z, core).
Axes of the slice: x: 4, y: 8, z: 8, core: 2. Of those that a mesh axis runs over, the one named last changes fastest.
Arguments:
- means: float32 [3, 262144], P(None, 'strip'), may hold values from -4 to 4
- inv_scales: float32 [2, 262144], P(None, 'strip'), may hold values from 0.15 to 0.6
- correlation: float32 [262144], P('strip'), may hold values from -0.6 to 0.6
- opacity: float32 [262144], P('strip'), may hold values from -7 to 4
- features: float32 [262144, 128], P('strip'), may hold values from -48 to 48
- cameras: float32 [4, 2, 4], P('view'), may hold values from -0.8 to 0.8
- owners: int32 [4, 128, 256, 1], P('view', 'strip'), may hold values from 0 to 127; in each aligned block of 256 rows (0 to 255, 256 to 511, ..., all dimensions but the last counted through in order) at most 4 rows name the same one
- slots: int32 [4, 128, 256], P('view', 'strip'), may hold values from 0 to 2047
- lengths: int32 [4, 128], P('view', 'strip'), may hold values from 1 to 256, 20480 in all within a row
- target: float32 [4, 2048, 16, 128], P('view', 'strip'), may hold values from -6 to 6
- weights: float32 [3, 3, 128, 128], replicated, may hold values from -0.1875 to 0.1875
- bias: float32 [128], replicated, may hold values from -3 to 3
Outputs:
- geometry_grad: float32 [7, 262144], P(None, 'strip')
- feature_grad: float32 [262144, 128], P('strip')
- weight_grad: float32 [3, 3, 128, 128], replicated
- bias_grad: float32 [128], replicated
Inputs may be any that keep to these rules, and one draw needn't show every extreme that they name: `owners`: in one device's entries (aligned blocks of 256 list entries in order of view, tile and position), no strip index is named more than 4 times; entries at or past a tile's length are padding but still name a primitive.
All inputs are finite; a program needn't handle non-finite values. No bound on the sum of `lengths` on one device may be relied on, other than what follows from the above.
Results may differ from a plain program's by a relative error of at most 0.0003.
Values sent between devices are 32-bit elements; how exact they have to be, the bound alone decides.
A program may use at most 64 MiB of HBM per device.

v0:
```python
import functools

import jax
import jax.numpy as jnp
from jax import lax
from jax.experimental import pallas as pl
from jax.experimental.pallas import tpu as pltpu
from jax.sharding import Mesh
from jax.sharding import PartitionSpec as P

STRIP = ("strip_0", "strip_1", "strip_2")
MESH = pl.DeviceIdType.MESH
F32 = jnp.float32
BF16 = jnp.bfloat16
RANKS = 4


def iota(shape, dim):
    return lax.broadcasted_iota(jnp.int32, shape, dim)


def mm(a, b, ca=1, cb=0):
    return lax.dot_general(a, b, (((ca,), (cb,)), ((), ())), preferred_element_type=F32)


def split(x):
    high = x.astype(BF16)
    return high, (x - high.astype(F32)).astype(BF16)


def split3(x):
    high = x.astype(BF16)
    rest = x - high.astype(F32)
    mid = rest.astype(BF16)
    return high, mid, (rest - mid.astype(F32)).astype(BF16)


def rows_of(ref, n):
    return ref.reshape(n, ref.shape[-1])[...]


def fill(ref, value):
    ref.reshape(*value.shape)[...] = value


def kernel(
    sizes,
    means, inv_scales, correlation, opacity, cameras, owners, slots, lengths, bias,
    features_hbm, target_hbm, weights_hbm,
    geometry_out, feature_out, weight_out, bias_out,
    feat, targ, wts, table, g_parts, f_parts, w_parts, w_turned, onehot, halo_t,
    req, req_mid, req_got, asked_all,
    geo, geo_mid, geo_got, fea, fea_mid, fea_got,
    image, back, back_mid, back_got, bgeo, bgeo_mid, bgeo_got, all_f, all_g,
    total, wl, wx, wc, wz, wz_got, wy, wy_got, wq, wq_got, wa, wfin,
    send, recv, local,
):
    nx, ny, nz, nc, entries, prims, height = sizes
    zc_count = nz * nc
    strips = ny * zc_count
    places = RANKS * strips
    width = 128
    pixels = height * 16
    extended = pixels + 32
    v = lax.axis_index("view")
    y = lax.axis_index("strip_0")
    z = lax.axis_index("strip_1")
    c = lax.axis_index("strip_2")
    zc = z * nc + c
    strip = y * zc_count + zc

    def at_zc(k):
        return (v, y, k // nc, k % nc)

    def at_y(k):
        return (v, k, z, c)

    def at_x(k):
        return (k, y, z, c)

    def at_strip(k):
        return (v, k // zc_count, (k % zc_count) // nc, k % nc)

    up = at_strip((strip + strips - 1) % strips)
    down = at_strip((strip + 1) % strips)

    def push(src, dst, n, device):
        pltpu.make_async_remote_copy(
            src_ref=src, dst_ref=dst, send_sem=send.at[n], recv_sem=recv.at[n],
            device_id=device, device_id_type=MESH,
        ).start()

    def keep(src, dst, n):
        pltpu.make_async_copy(src, dst, recv.at[n]).start()

    def landed(ref, n):
        pltpu.make_async_copy(ref, ref, recv.at[n]).wait()

    def sent(ref, n):
        pltpu.make_async_copy(ref, ref, send.at[n]).wait()

    pending = []

    def to_zc(src, dst, n):
        @pl.loop(1, zc_count)
        def _(j):
            k = (zc + j) % zc_count
            push(src.at[:, k], dst.at[:, zc], n, at_zc(k))

        keep(src.at[:, zc], dst.at[:, zc], n)
        pending.append((src.at[:, 0 : zc_count - 1], n))

    def to_y(src, dst, n):
        @pl.loop(1, ny)
        def _(j):
            k = (y + j) % ny
            push(src.at[:, :, k], dst.at[:, :, y], n, at_y(k))

        keep(src.at[:, :, y], dst.at[:, :, y], n)
        pending.append((src.at[:, :, 0 : ny - 1], n))

    load_f = pltpu.make_async_copy(features_hbm, feat, local.at[0])
    load_t = pltpu.make_async_copy(target_hbm, targ, local.at[1])
    load_w = pltpu.make_async_copy(weights_hbm, wts, local.at[2])
    load_f.start()
    load_t.start()
    load_w.start()

    barrier = pltpu.get_barrier_semaphore()

    @pl.loop(1, zc_count)
    def _(j):
        pl.semaphore_signal(barrier, inc=1, device_id=at_zc((zc + j) % zc_count), device_id_type=MESH)

    @pl.loop(1, ny)
    def _(j):
        pl.semaphore_signal(barrier, inc=1, device_id=at_y((y + j) % ny), device_id_type=MESH)

    @pl.loop(1, nx)
    def _(j):
        pl.semaphore_signal(barrier, inc=1, device_id=at_x((v + j) % nx), device_id_type=MESH)

    pl.semaphore_signal(barrier, inc=1, device_id=up, device_id_type=MESH)
    pl.semaphore_signal(barrier, inc=1, device_id=down, device_id_type=MESH)

    def column(row):
        n = row.shape[1]
        same = iota((n, n), 0) == iota((n, n), 1)
        return jnp.sum(jnp.where(same, jnp.broadcast_to(row, (n, n)), 0.0), axis=1, keepdims=True)

    owner = owners[...]
    home = ((owner % zc_count) * ny + owner // zc_count).astype(F32)
    home_col = column(home)
    slot_col = column(slots[...].astype(F32))
    alike = home_col == home
    first = iota((entries, entries), 0)
    second = iota((entries, entries), 1)
    rank_col = jnp.sum(jnp.where(alike & (second < first), 1.0, 0.0), axis=1, keepdims=True)
    rank_row = jnp.sum(jnp.where(alike & (first < second), 1.0, 0.0), axis=0, keepdims=True)
    at_home = jnp.where(iota((strips, entries), 0).astype(F32) == home, 1.0, 0.0).astype(BF16)
    lane = iota((entries, width), 1).astype(F32)
    slot_high = jnp.floor(slot_col * (1.0 / 64.0))
    slot_low = slot_col - 64.0 * slot_high
    in_rank = lane == rank_col
    asked_high = mm(at_home, jnp.where(in_rank, slot_high, 0.0).astype(BF16))
    asked_low = mm(at_home, jnp.where(in_rank, slot_low, 0.0).astype(BF16))
    fill(req, asked_high * 64.0 + asked_low)

    pl.semaphore_wait(barrier, zc_count + ny + nx - 3 + 2)

    to_zc(req, req_mid, 0)
    push(target_hbm.at[0:16], halo_t.at[1], 1, up)
    push(target_hbm.at[pixels - 16 : pixels], halo_t.at[0], 1, down)
    pending.append((halo_t, 1))

    table[0:3, :] = means[...]
    table[3:5, :] = inv_scales[...]
    table[5:6, :] = correlation[...]
    table[6:7, :] = opacity[...]
    table[7:8, :] = jnp.zeros((1, prims), F32)
    whole = table[...]
    g_high, g_mid, g_low = (part.astype(F32) for part in split3(whole))
    g_parts[...] = jnp.concatenate(
        [g_high] * RANKS + [g_mid] * RANKS + [g_low] * RANKS + [jnp.zeros((32, prims), F32)], axis=0
    ).astype(BF16)
    load_f.wait()
    rows = min(prims, 256)

    @pl.loop(0, prims // rows)
    def _(i):
        here = pl.ds(pl.multiple_of(i * rows, rows), rows)
        high, low = split(feat[here, :])
        f_parts[here, 0:width] = high
        f_parts[here, width : 2 * width] = low

    landed(req_mid, 0)
    to_y(req_mid, req_got, 2)

    load_w.wait()
    for tap in range(9):
        high, low = split(wts[tap * width : (tap + 1) * width, :])
        w_parts[tap * width : (tap + 1) * width, 0:width] = high
        w_parts[tap * width : (tap + 1) * width, width : 2 * width] = low
        a, b = 2 - tap // 3, 2 - tap % 3
        w_turned[a, 0, :, b * width : (b + 1) * width] = high
        w_turned[a, 1, :, b * width : (b + 1) * width] = low
    load_t.wait()

    landed(req_got, 2)
    asked = rows_of(req_got, strips)
    square = jnp.concatenate([asked, jnp.zeros((width - strips, width), F32)], axis=0) if strips < width else asked
    asked_rows = jnp.transpose(square)[0:8, 0:strips]
    asked_all[v] = asked_rows

    @pl.loop(1, nx)
    def _(j):
        push(asked_all.at[v], asked_all.at[v], 3, at_x((v + j) % nx))

    if nx > 1:
        pending.append((asked_all.at[0 : nx - 1], 3))

    ident = iota((strips, prims), 1).astype(F32)
    packed = jnp.zeros((strips, width), F32)
    lanes = iota((strips, width), 1)
    for r in range(RANKS):
        onehot[r * strips : (r + 1) * strips, :] = jnp.where(ident == asked[:, r : r + 1], 1.0, 0.0).astype(BF16)
    for r in range(RANKS):
        found = mm(onehot[r * strips : (r + 1) * strips, :], g_parts[...], 1, 1)
        packed = packed + jnp.where((lanes % 32) // 8 == r, found, 0.0)

    def folded(x):
        x = x + pltpu.roll(x, width - 32, 1) + pltpu.roll(x, width - 64, 1)
        return jnp.where(lanes < 32, x, 0.0)

    fill(geo, folded(packed))
    to_zc(geo, geo_mid, 4)

    @pl.loop(0, RANKS)
    def _(r):
        here = pl.ds(pl.multiple_of(r * strips, strips), strips)
        found = mm(onehot[here, :], f_parts[...])
        fill(fea.at[r], found[:, 0:width] + found[:, width : 2 * width])

    half = RANKS // 2
    to_zc(fea.at[0:half], fea_mid.at[0:half], 5)
    to_y(fea.at[half:RANKS], fea_mid.at[half:RANKS], 6)

    landed(geo_mid, 4)
    to_y(geo_mid, geo_got, 7)

    place_row = rank_row * float(strips) + home
    place_col = rank_col * float(strips) + home_col
    to_place = jnp.where(iota((places, entries), 0).astype(F32) == place_row, 1.0, 0.0).astype(BF16)
    from_place = jnp.where(iota((entries, places), 1).astype(F32) == place_col, 1.0, 0.0).astype(BF16)
    before = jnp.where(first < second, 1.0, 0.0).astype(BF16)
    behind = jnp.where(first > second, 1.0, 0.0).astype(BF16)

    landed(fea_mid.at[0:half], 5)
    to_y(fea_mid.at[0:half], fea_got.at[0:half], 8)
    landed(fea_mid.at[half:RANKS], 6)
    to_zc(fea_mid.at[half:RANKS], fea_got.at[half:RANKS], 9)

    landed(geo_got, 7)

    def turned(x):
        x = jnp.concatenate([x, jnp.zeros((width - strips, width), F32)], axis=0) if strips < width else x
        return jnp.transpose(x)[0 : 8 * RANKS, 0:strips]

    def three(x):
        return jnp.concatenate([part.astype(F32) for part in split3(x)], axis=0).astype(BF16)

    spread = mm(three(turned(rows_of(geo_got, strips))), at_home)
    n8 = 8 * RANKS
    spread = spread[0:n8] + spread[n8 : 2 * n8] + spread[2 * n8 : 3 * n8]
    g = jnp.zeros((8, entries), F32)
    for r in range(RANKS):
        g = g + jnp.where(rank_row == float(r), spread[8 * r : 8 * r + 8, :], 0.0)

    def cam(axis, k):
        return cameras[0, axis * 4 + k]

    def center(axis):
        return 8.0 + 4.0 * (
            cam(axis, 0) * g[0:1] + cam(axis, 1) * g[1:2] + cam(axis, 2) * g[2:3] + cam(axis, 3)
        )

    pixel = iota((pixels, 1), 0)
    across = (pixel % 16).astype(F32) + 0.5
    downward = (pixel // 16).astype(F32) + 0.5
    du = across - center(0)
    dv = downward - center(1)
    a = g[3:4] * du
    b = g[4:5] * dv
    skew = g[5:6]
    grown = jnp.exp(-0.5 * (a * a + 2.0 * skew * a * b + b * b))
    solid = 1.0 / (1.0 + jnp.exp(-g[6:7]))
    raw = solid * grown
    alive = jnp.where(iota((1, entries), 1) < lengths[0, 0], 1.0, 0.0)
    cover = jnp.minimum(raw, 0.99) * alive
    fades = jnp.log(1.0 - cover)
    f_high, f_mid, f_low = split3(fades)
    through = jnp.exp(mm(f_high, before) + mm(f_mid, before) + mm(f_low, before))
    weight = cover * through
    weight_high, weight_low = split(weight)

    landed(fea_got.at[0:half], 8)
    landed(fea_got.at[half:RANKS], 9)
    high, low = split(rows_of(fea_got, places))
    listed = mm(from_place, jnp.concatenate([high, low], axis=1)).astype(BF16)
    both = mm(weight_high, listed)
    image[32 : 32 + pixels, :] = both[:, 0:width] + both[:, width:] + mm(weight_low, listed[:, 0:width])

    push(image.at[32:64], image.at[32 + pixels : 64 + pixels], 10, up)
    push(image.at[pixels : 32 + pixels], image.at[0:32], 10, down)
    pending.append((image.at[0:64], 10))
    landed(image.at[0:64], 10)
    landed(halo_t, 1)

    has_up = strip > 0
    has_down = strip < strips - 1
    rows_at = iota((pixels + 64, 1), 0)
    inside = ((rows_at >= 32) | has_up) & ((rows_at < 32 + pixels) | has_down)
    pic = jnp.where(inside, image[...], 0.0)

    def sideways(x):
        n = x.shape[0]
        col = iota((n, 1), 0) % 16
        left = jnp.where(col == 0, 0.0, pltpu.roll(x, 1, 0))
        right = jnp.where(col == 15, 0.0, pltpu.roll(x, n - 1, 0))
        return split(jnp.concatenate([left, x, right], axis=1))

    pic_high, pic_low = sideways(pic)
    decoded = jnp.zeros((extended, 2 * width), F32)
    rest = jnp.zeros((extended, width), F32)
    for i in range(3):
        part = w_parts[i * 3 * width : (i + 1) * 3 * width, :]
        decoded = decoded + mm(pic_high[i * 16 : i * 16 + extended, :], part)
        rest = rest + mm(pic_low[i * 16 : i * 16 + extended, :], part[:, 0:width])
    decoded = decoded[:, 0:width] + (decoded[:, width:] + rest) + bias[...]
    aim = jnp.concatenate([halo_t[0], targ[...], halo_t[1]], axis=0)
    rows_at = iota((extended, 1), 0)
    inside = ((rows_at >= 16) | has_up) & ((rows_at < 16 + pixels) | has_down)
    residual = jnp.where(inside, decoded - aim, 0.0)
    res_high, res_low = sideways(residual)
    grad = jnp.zeros((pixels, width), F32)
    for i in range(3):
        here = slice(i * 16, i * 16 + pixels)
        grad = grad + (
            mm(res_high[here, :], w_turned[i, 0], 1, 1)
            + (mm(res_high[here, :], w_turned[i, 1], 1, 1) + mm(res_low[here, :], w_turned[i, 0], 1, 1))
        )
    grad_high, grad_low = split(grad)

    both = mm(weight_high, jnp.concatenate([grad_high, grad_low], axis=1), 0, 0)
    f_grad = both[:, 0:width] + (both[:, width:] + mm(weight_low, grad_high, 0, 0))
    high, low = split(f_grad)
    both = mm(to_place, jnp.concatenate([high, low], axis=1))
    fill(back, both[:, 0:width] + both[:, width:])
    to_zc(back.at[0:half], back_mid.at[0:half], 11)
    to_y(back.at[half:RANKS], back_mid.at[half:RANKS], 12)

    own = residual[16 : 16 + pixels, :]
    shifted = []
    for i in range(3):
        shifted.append(
            jnp.concatenate(
                [jnp.zeros(((i + 1) * 16, width), F32), own, jnp.zeros((64 - (i + 1) * 16, width), F32)], axis=0
            )
        )
    own_high, own_low = split(jnp.concatenate(shifted, axis=1))
    w_grad = mm(pic_high, own_high, 0, 0) + (mm(pic_high, own_low, 0, 0) + mm(pic_low, own_high, 0, 0))
    for i in range(3):
        wl[i * 3 * width : (i + 1) * 3 * width, :] = w_grad[:, i * width : (i + 1) * width]
    b_grad = jnp.broadcast_to(jnp.sum(own, axis=0, keepdims=True), (8, width))
    per_z = 9 * width // zc_count
    per_y = per_z // ny
    for k in range(zc_count):
        wx[k // nz, k % nz, 0:per_z, :] = wl[k * per_z : (k + 1) * per_z, :]
        wx[k // nz, k % nz, per_z : per_z + 8, :] = b_grad
    other = (v, y, z, 1 - c)
    push(wx.at[1 - c], wc, 13, other)
    pending.append((wc, 13))

    d_weight = mm(jnp.concatenate([grad_high, grad_high], axis=1), listed, 1, 1) + mm(
        grad_low, listed[:, 0:width], 1, 1
    )
    f_high, f_mid, f_low = split3(d_weight * weight)
    later = mm(f_high, behind) + mm(f_mid, behind) + mm(f_low, behind)
    d_cover = d_weight * through - later / (1.0 - cover)
    d_raw = jnp.where(raw < 0.99, d_cover, 0.0) * alive
    d_grown = d_raw * raw
    u = (a + skew * b) * d_grown
    w = (b + skew * a) * d_grown

    def summed(x):
        return jnp.sum(x, axis=0, keepdims=True)

    d_col = 4.0 * g[3:4] * summed(u)
    d_row = 4.0 * g[4:5] * summed(w)
    parts = [cam(0, k) * d_col + cam(1, k) * d_row for k in range(3)]
    parts += [-summed(u * du), -summed(w * dv), -summed(d_grown * a * b), summed(d_grown) * (1.0 - solid)]
    parts.append(jnp.zeros((1, entries), F32))
    g_grad = jnp.concatenate(parts, axis=0)
    by_rank = jnp.concatenate([jnp.where(rank_row == float(r), g_grad, 0.0) for r in range(RANKS)], axis=0)
    by_rank = jnp.concatenate([part.astype(F32) for part in split3(by_rank)] + [jnp.zeros((32, entries), F32)], axis=0)
    fill(bgeo, folded(mm(at_home, by_rank.astype(BF16), 1, 1)))
    to_zc(bgeo, bgeo_mid, 14)

    landed(wc, 13)
    wz[...] = wx[c] + wc[...]

    @pl.loop(1, nz)
    def _(j):
        k = (z + j) % nz
        push(wz.at[k], wz_got.at[z], 15, (v, y, k, c))

    keep(wz.at[z], wz_got.at[z], 15)
    pending.append((wz.at[0 : nz - 1], 15))

    landed(back_mid.at[0:half], 11)
    to_y(back_mid.at[0:half], back_got.at[0:half], 16)
    landed(back_mid.at[half:RANKS], 12)
    to_zc(back_mid.at[half:RANKS], back_got.at[half:RANKS], 17)
    landed(bgeo_mid, 14)
    to_y(bgeo_mid, bgeo_got, 18)

    landed(wz_got, 15)
    sums = wz_got[0]
    for k in range(1, nz):
        sums = sums + wz_got[k]
    for k in range(ny):
        fill(wy.at[k, 0:per_y], sums[k * per_y : (k + 1) * per_y, :])
        fill(wy.at[k, per_y : per_y + 1], sums[per_z : per_z + 1, :])

    @pl.loop(1, ny)
    def _(j):
        k = (y + j) % ny
        push(wy.at[k], wy_got.at[y], 19, at_y(k))

    keep(wy.at[y], wy_got.at[y], 19)
    pending.append((wy.at[0 : ny - 1], 19))

    def to_x(src, dst, n):
        @pl.loop(1, nx)
        def _(j):
            push(src, dst, n, at_x((v + j) % nx))

        keep(src, dst, n)
        for _ in range(nx - 1):
            pending.append((src, n))

    landed(back_got.at[0:half], 16)
    to_x(back_got.at[0:half], all_f.at[v, 0:half], 20)
    landed(back_got.at[half:RANKS], 17)
    to_x(back_got.at[half:RANKS], all_f.at[v, half:RANKS], 21)
    landed(bgeo_got, 18)
    to_x(bgeo_got, all_g.at[v], 22)

    landed(wy_got, 19)
    sums = wy_got[0]
    for k in range(1, ny):
        sums = sums + wy_got[k]
    wq[...] = sums
    to_x(wq, wq_got.at[v], 23)

    if nx > 1:
        landed(asked_all.at[0 : nx - 1], 3)
    landed(wq_got, 23)
    sums = wq_got[0]
    for k in range(1, nx):
        sums = sums + wq_got[k]
    bias_out[...] = sums[per_y]
    wa[y] = sums[0:per_y]

    @pl.loop(1, ny)
    def _(j):
        push(wa.at[y], wa.at[y], 24, at_y((y + j) % ny))

    pending.append((wa.at[0 : ny - 1], 24))

    slot_at = iota((rows, 1), 0).astype(F32)

    def scatter(r0, r1):
        @pl.loop(0, nx)
        def _(view):
            asks = asked_all[view]
            asks = jnp.concatenate([asks[r : r + 1, :] for r in range(r0, r1)], axis=1)
            high, low = split(rows_of(all_f.at[view, r0:r1], (r1 - r0) * strips))
            came = jnp.concatenate([high, low], axis=1)

            @pl.loop(0, prims // rows)
            def _(i):
                start = pl.multiple_of(i * rows, rows)
                here = pl.ds(start, rows)
                hits = jnp.where(slot_at + (i * rows).astype(F32) == asks, 1.0, 0.0).astype(BF16)
                both = mm(hits, came)
                both = both[:, 0:width] + both[:, width:]
                total[here, :] += both

    landed(all_f.at[:, 0:half], 20)
    total[...] = jnp.zeros((prims, width), F32)
    scatter(0, half)

    if ny > 1:
        landed(wa.at[0 : ny - 1], 24)
    wfin[c, z] = rows_of(wa, per_z)

    @pl.loop(1, nz)
    def _(j):
        push(wfin.at[c, z], wfin.at[c, z], 25, (v, y, (z + j) % nz, c))

    if nz > 1:
        pending.append((wfin.at[c, 0 : nz - 1], 25))

    landed(all_f.at[:, half:RANKS], 21)
    scatter(half, RANKS)
    save_f = pltpu.make_async_copy(total, feature_out, local.at[3])
    save_f.start()

    if nz > 1:
        landed(wfin.at[c, 0 : nz - 1], 25)
    push(wfin.at[c], wfin.at[c], 26, other)
    pending.append((wfin.at[c], 26))

    landed(all_g, 22)

    def geometry_of(view):
        pieces = turned(rows_of(all_g.at[view], strips))
        pieces = jnp.concatenate([pieces[8 * r : 8 * r + 8, :] for r in range(RANKS)], axis=1)
        return three(pieces)

    came_g = [geometry_of(view) for view in range(nx)]
    asks_g = [
        jnp.concatenate([asked_all[view][r : r + 1, :] for r in range(RANKS)], axis=1) for view in range(nx)
    ]
    for i in range(prims // rows):
        acc = jnp.zeros((24, rows), F32)
        for view in range(nx):
            hits = jnp.where(slot_at + float(i * rows) == asks_g[view], 1.0, 0.0).astype(BF16)
            acc = acc + mm(came_g[view], hits, 1, 1)
        acc = acc[0:8] + acc[8:16] + acc[16:24]
        geometry_out[:, i * rows : (i + 1) * rows] = acc[0:7]

    landed(wfin.at[0], 26)
    save_w = pltpu.make_async_copy(wfin, weight_out, local.at[4])
    save_w.start()
    for ref, n in pending:
        sent(ref, n)
    save_f.wait()
    save_w.wait()


def per_device(sizes, *arrays):
    means, inv_scales, correlation, opacity, features, cameras, owners, slots, lengths, target, weights, bias = arrays
    nx, ny, nz, nc, entries, prims, height = sizes
    zc = nz * nc
    strips = ny * zc
    width = 128
    pixels = height * 16
    per_z = 9 * width // zc
    per_y = per_z // ny
    vmem = pl.BlockSpec(memory_space=pltpu.VMEM)
    smem = pl.BlockSpec(memory_space=pltpu.SMEM)
    any_ = pl.BlockSpec(memory_space=pl.ANY)

    def f32(*shape):
        return pltpu.VMEM(shape, F32)

    def planes(n):
        return f32(n, zc, ny, 1, width)

    geometry, feature, weight, b_grad = pl.pallas_call(
        functools.partial(kernel, sizes),
        name="splat_step",
        out_shape=(
            jax.ShapeDtypeStruct((7, prims), F32),
            jax.ShapeDtypeStruct((prims, width), F32),
            jax.ShapeDtypeStruct((nc, nz, per_z, width), F32),
            jax.ShapeDtypeStruct((1, width), F32),
        ),
        in_specs=[vmem] * 4 + [smem, vmem, vmem, smem, vmem] + [any_] * 3,
        out_specs=(vmem, any_, any_, vmem),
        scratch_shapes=[
            f32(prims, width), f32(pixels, width), f32(9 * width, width), f32(8, prims),
            pltpu.VMEM((width, prims), BF16), pltpu.VMEM((prims, 2 * width), BF16),
            pltpu.VMEM((9 * width, 2 * width), BF16), pltpu.VMEM((3, 2, width, 3 * width), BF16),
            pltpu.VMEM((RANKS * strips, prims), BF16), f32(2, 16, width),
            planes(1), planes(1), planes(1), f32(nx, 8, strips),
            planes(1), planes(1), planes(1), planes(RANKS), planes(RANKS), planes(RANKS),
            f32(pixels + 64, width), planes(RANKS), planes(RANKS), planes(RANKS), planes(1), planes(1), planes(1),
            f32(nx, RANKS, zc, ny, 1, width), f32(nx, 1, zc, ny, 1, width),
            f32(prims, width), f32(9 * width, width), f32(nc, nz, per_z + 8, width), f32(nz, per_z + 8, width),
            f32(nz, per_z + 8, width), f32(nz, per_z + 8, width),
            f32(ny, per_y + 1, 1, width), f32(ny, per_y + 1, 1, width), f32(per_y + 1, 1, width),
            f32(nx, per_y + 1, 1, width), f32(ny, per_y, 1, width), f32(nc, nz, per_z, width),
            pltpu.SemaphoreType.DMA((27,)), pltpu.SemaphoreType.DMA((27,)), pltpu.SemaphoreType.DMA((5,)),
        ],
        compiler_params=pltpu.CompilerParams(
            collective_id=0, has_side_effects=True, vmem_limit_bytes=56 * 1024 * 1024
        ),
    )(
        means, inv_scales, correlation.reshape(1, prims), opacity.reshape(1, prims), cameras.reshape(1, 8),
        owners.reshape(1, entries), slots.reshape(1, entries), lengths.reshape(1, 1), bias.reshape(1, width),
        features, target.reshape(pixels, width), weights.reshape(9 * width, width),
    )
    return geometry, feature, weight.reshape(3, 3, width, width), b_grad.reshape(width)


def built(mesh, ny, nz, nc, entries, prims, height):
    nx = mesh.shape["view"]
    finer = Mesh(mesh.devices.reshape(nx, ny, nz, nc), ("view",) + STRIP)
    return jax.shard_map(
        functools.partial(per_device, (nx, ny, nz, nc, entries, prims, height)),
        mesh=finer,
        in_specs=(
            P(None, STRIP),
            P(None, STRIP),
            P(STRIP),
            P(STRIP),
            P(STRIP, None),
            P("view", None, None),
            P("view", STRIP, None, None),
            P("view", STRIP, None),
            P("view", STRIP),
            P("view", STRIP, None, None),
            P(),
            P(),
        ),
        out_specs=(P(None, STRIP), P(STRIP, None), P(), P()),
        check_vma=False,
    )


def solution(mesh):
    return built(mesh, 8, 8, 2, 256, 2048, 16)
```

profile of v0, /device:TPU:1, one launch (start us, length us, event | category | flops | bytes accessed | tf_op | source)
XLA Modules:
  0.0 103.2 jit_solution(17927624477232143515)
XLA Ops:
  1.3 0.0 copy-start.1
  1.3 0.7 copy-done.1
  2.0 0.6 reshape.40.cameras
  2.5 95.5 %splat_step.1 = (f32[7,2048]{1,0:T(8,128)}, f32[2048,128]{1,0:T(8,128)}, f32[2,8,72,128]{3,2,1,0:T(8,128)}, f32[1,128]{1,0:T(1,128)}) custom-call(f32[3,2048]{1,0:T(4,128)} %means.1, f32[2,2048]{1,0:T(2,128)} %inv_scales.1, f32[1,2048]{1,0:T(1,128)} %bitcast.12, f32[1,2048]{1,0:T(1,128)} %bitcast.13, f32[1,8]{1,0:T(1,128)} %reshape.40.cameras, ...), custom_call_target="tpu_custom_call" | custom-call | tf_op jit(solution)/shard_map/splat_step/pallas_call | solution.py:572
  98.0 1.5 %copy.21 = f32[7,2048]{1,0:T(8,128)} copy(f32[7,2048]{1,0:T(8,128)} %get-tuple-element.16) | data formatting | bytes 114688
  99.5 0.0 copy-start
  99.5 2.3 %copy.22 = f32[2048,128]{1,0:T(8,128)} copy(f32[2048,128]{1,0:T(8,128)} %get-tuple-element.17) | data formatting | bytes 2097152
  101.8 0.0 copy-done
  101.8 0.0 copy-start.2
  101.8 0.8 copy.23
  102.7 0.0 copy-done.2
  102.7 0.5 copy.24
Async XLA Ops:
  1.3 0.7 copy-start.1
  99.5 2.3 %copy-start = (f32[2,8,72,128]{3,2,1,0:T(8,128)S(1)}, f32[2,8,72,128]{3,2,1,0:T(8,128)}, u32[]{:S(2)}) copy-start(f32[2,8,72,128]{3,2,1,0:T(8,128)} %get-tuple-element.10) | copy-start | bytes 1769476
  101.8 0.8 copy-start.2
where the time goes:
time: 105 us; the launch traced here: 103 us
  Pallas kernels  95.5 us (91%)
  local copies, waits for them, and re-layouts  6.39 us (6%)
  between operations  1.3 us (1%)
    pallas_call x1, Pallas kernels, per_device(): pl.pallas_call(functools.partial(kernel, sizes), name='splat_step', out_s...  95.5 us
    unnamed x10, local copies, waits for them, and re-layouts  5.8 us

commit v1 on v0

v1 whole, which is shorter than its diff:
```python
import functools

import jax
import jax.numpy as jnp
from jax import lax
from jax.experimental import pallas as pl
from jax.experimental.pallas import tpu as pltpu
from jax.sharding import Mesh
from jax.sharding import PartitionSpec as P

STRIP = ("strip_0", "strip_1", "strip_2")
MESH = pl.DeviceIdType.MESH
F32 = jnp.float32
BF16 = jnp.bfloat16
VMEM_LIMIT = 24 * 1024 * 1024
RANKS = 4


def iota(shape, dim):
    return lax.broadcasted_iota(jnp.int32, shape, dim)


def mm(a, b, ca=1, cb=0):
    return lax.dot_general(a, b, (((ca,), (cb,)), ((), ())), preferred_element_type=F32)


def split(x):
    high = x.astype(BF16)
    return high, (x - high.astype(F32)).astype(BF16)


def split3(x):
    high = x.astype(BF16)
    rest = x - high.astype(F32)
    mid = rest.astype(BF16)
    return high, mid, (rest - mid.astype(F32)).astype(BF16)


def rows_of(ref, n):
    return ref.reshape(n, ref.shape[-1])[...]


def fill(ref, value):
    ref.reshape(*value.shape)[...] = value


def kernel(
    sizes,
    means, inv_scales, correlation, opacity, cameras, owners_hbm, slots_hbm, lengths, bias_hbm,
    features_hbm, target_hbm, weights_hbm,
    geometry_out, feature_out, weight_out, bias_out,
    owners, slots, bias, feat, targ, wts, table, g_parts, f_parts, w_parts, w_turned, onehot, halo_t,
    req, req_mid, req_got, asked_all,
    geo, geo_mid, geo_got, fea, fea_mid, fea_got,
    image, back, back_mid, back_got, bgeo, bgeo_mid, bgeo_got, all_f, all_g,
    total, total_g, wl, wx, wc, wa, wa_got, wb, wb_got, wa2, wa2_got, wb2, wb2_got, wq, wq_got, wa3, wb3, wfin,
    send, recv, local,
):
    nx, ny, nz, nc, entries, prims, height = sizes
    zc_count = nz * nc
    strips = ny * zc_count
    places = RANKS * strips
    width = 128
    pixels = height * 16
    extended = pixels + 32
    v = lax.axis_index("view")
    y = lax.axis_index("strip_0")
    z = lax.axis_index("strip_1")
    c = lax.axis_index("strip_2")
    zc = z * nc + c
    strip = y * zc_count + zc

    def at_zc(k):
        return (v, y, k // nc, k % nc)

    def at_y(k):
        return (v, k, z, c)

    def at_x(k):
        return (k, y, z, c)

    def at_strip(k):
        return (v, k // zc_count, (k % zc_count) // nc, k % nc)

    up = at_strip((strip + strips - 1) % strips)
    down = at_strip((strip + 1) % strips)

    def push(src, dst, n, device):
        pltpu.make_async_remote_copy(
            src_ref=src, dst_ref=dst, send_sem=send.at[n], recv_sem=recv.at[n],
            device_id=device, device_id_type=MESH,
        ).start()

    def keep(src, dst, n):
        pltpu.make_async_copy(src, dst, recv.at[n]).start()

    def landed(ref, n):
        pltpu.make_async_copy(ref, ref, recv.at[n]).wait()

    def sent(ref, n):
        pltpu.make_async_copy(ref, ref, send.at[n]).wait()

    pending = []

    def drain():
        for ref, n in pending:
            sent(ref, n)
        pending.clear()

    def to_zc(src, dst, n):
        for j in range(1, zc_count):
            k = (zc + j) % zc_count
            push(src.at[:, k], dst.at[:, zc], n, at_zc(k))

        keep(src.at[:, zc], dst.at[:, zc], n)
        if zc_count > 1:
            pending.append((src.at[:, 0 : zc_count - 1], n))

    def to_y(src, dst, n):
        for j in range(1, ny):
            k = (y + j) % ny
            push(src.at[:, :, k], dst.at[:, :, y], n, at_y(k))

        keep(src.at[:, :, y], dst.at[:, :, y], n)
        if ny > 1:
            pending.append((src.at[:, :, 0 : ny - 1], n))

    load_o = pltpu.make_async_copy(owners_hbm, owners, local.at[5])
    load_s = pltpu.make_async_copy(slots_hbm, slots, local.at[6])
    load_b = pltpu.make_async_copy(bias_hbm, bias, local.at[7])
    load_g = [
        pltpu.make_async_copy(ref, table.at[a:b], local.at[8 + i])
        for i, (ref, a, b) in enumerate(
            ((means, 0, 3), (inv_scales, 3, 5), (correlation, 5, 6), (opacity, 6, 7))
        )
    ]
    load_o.start()
    load_s.start()
    load_f = pltpu.make_async_copy(features_hbm, feat, local.at[0])
    load_t = pltpu.make_async_copy(target_hbm, targ, local.at[1])
    load_w = pltpu.make_async_copy(weights_hbm, wts, local.at[2])

    barrier = pltpu.get_barrier_semaphore()

    for j in range(1, zc_count):
        pl.semaphore_signal(barrier, inc=1, device_id=at_zc((zc + j) % zc_count), device_id_type=MESH)

    for j in range(1, ny):
        pl.semaphore_signal(barrier, inc=1, device_id=at_y((y + j) % ny), device_id_type=MESH)

    for j in range(1, nx):
        pl.semaphore_signal(barrier, inc=1, device_id=at_x((v + j) % nx), device_id_type=MESH)

    pl.semaphore_signal(barrier, inc=1, device_id=up, device_id_type=MESH)
    pl.semaphore_signal(barrier, inc=1, device_id=down, device_id_type=MESH)

    for load in load_g + [load_f, load_t, load_w, load_b]:
        load.start()

    def column(row):
        n = row.shape[1]
        same = iota((n, n), 0) == iota((n, n), 1)
        return jnp.sum(jnp.where(same, jnp.broadcast_to(row, (n, n)), 0.0), axis=1, keepdims=True)

    first = iota((entries, entries), 0)
    second = iota((entries, entries), 1)
    load_o.wait()
    owner = owners[...]
    home = ((owner % zc_count) * ny + owner // zc_count).astype(F32)
    home_col = column(home)
    alike = home_col == home
    rank_row = jnp.sum(jnp.where(alike & (first < second), 1.0, 0.0), axis=0, keepdims=True)
    at_home = jnp.where(iota((strips, entries), 0).astype(F32) == home, 1.0, 0.0).astype(BF16)
    load_s.wait()
    slot = slots[...].astype(F32)
    slot_high = jnp.floor(slot * (1.0 / 64.0))
    slot_low = slot - 64.0 * slot_high
    row_at = iota((width, entries), 0).astype(F32)
    sought = jnp.where(row_at == rank_row, slot_high, 0.0) + jnp.where(row_at - 8.0 == rank_row, slot_low, 0.0)
    sought = mm(at_home, sought.astype(BF16), 1, 1)
    fill(req, sought * 64.0 + pltpu.roll(sought, width - 8, 1))

    pl.semaphore_wait(barrier, zc_count + ny + nx - 3 + 2)

    to_zc(req, req_mid, 0)
    push(target_hbm.at[0:16], halo_t.at[1], 1, up)
    push(target_hbm.at[pixels - 16 : pixels], halo_t.at[0], 1, down)
    pending.append((halo_t, 1))

    for load in load_g:
        load.wait()
    whole = jnp.concatenate([table[...], jnp.zeros((1, prims), F32)], axis=0)
    g_high, g_mid, g_low = (part.astype(F32) for part in split3(whole))
    g_parts[...] = jnp.concatenate(
        [g_high] * RANKS + [g_mid] * RANKS + [g_low] * RANKS + [jnp.zeros((32, prims), F32)], axis=0
    ).astype(BF16)
    load_f.wait()
    rows = min(prims, 512)

    @pl.loop(0, prims // rows)
    def _(i):
        here = pl.ds(pl.multiple_of(i * rows, rows), rows)
        high, low = split(feat[here, :])
        f_parts[here, 0:width] = high
        f_parts[here, width : 2 * width] = low

    landed(req_mid, 0)
    to_y(req_mid, req_got, 2)

    load_w.wait()
    for tap in range(9):
        high, low = split(wts[tap * width : (tap + 1) * width, :])
        w_parts[tap * width : (tap + 1) * width, 0:width] = high
        w_parts[tap * width : (tap + 1) * width, width : 2 * width] = low
        a, b = 2 - tap // 3, 2 - tap % 3
        w_turned[a, 0, :, b * width : (b + 1) * width] = high
        w_turned[a, 1, :, b * width : (b + 1) * width] = low
    load_t.wait()
    load_b.wait()
    rank_col = jnp.sum(jnp.where(alike & (second < first), 1.0, 0.0), axis=1, keepdims=True)
    place_row = rank_row * float(strips) + home
    place_col = rank_col * float(strips) + home_col
    to_place = jnp.where(iota((places, entries), 0).astype(F32) == place_row, 1.0, 0.0).astype(BF16)
    from_place = jnp.where(iota((entries, places), 1).astype(F32) == place_col, 1.0, 0.0).astype(BF16)
    before = jnp.where(first < second, 1.0, 0.0).astype(BF16)
    behind = jnp.where(first > second, 1.0, 0.0).astype(BF16)

    landed(req_got, 2)
    asked = rows_of(req_got, strips)
    square = jnp.concatenate([asked, jnp.zeros((width - strips, width), F32)], axis=0) if strips < width else asked
    asked_rows = jnp.transpose(square)[0:8, 0:strips]
    asked_all[v] = asked_rows

    for j in range(1, nx):
        push(asked_all.at[v], asked_all.at[v], 3, at_x((v + j) % nx))

    if nx > 1:
        pending.append((asked_all.at[0 : nx - 1], 3))

    block = min(prims, 256)
    ident = iota((1, block), 1).astype(F32).astype(BF16)
    packed = jnp.zeros((strips, width), F32)
    lanes = iota((strips, width), 1)
    for r in range(RANKS):
        for k in range(prims // block):
            near = (asked[:, r : r + 1] - float(k * block)).astype(BF16)
            onehot[r * strips : (r + 1) * strips, k * block : (k + 1) * block] = jnp.where(
                ident == near, jnp.ones((), BF16), jnp.zeros((), BF16)
            )
    for r in range(RANKS):
        found = mm(onehot[r * strips : (r + 1) * strips, :], g_parts[...], 1, 1)
        packed = packed + jnp.where((lanes % 32) // 8 == r, found, 0.0)

    def folded(x):
        x = x + pltpu.roll(x, width - 32, 1) + pltpu.roll(x, width - 64, 1)
        return jnp.where(lanes < 32, x, 0.0)

    fill(geo, folded(packed))
    to_zc(geo, geo_mid, 4)

    for r in range(RANKS):
        found = mm(onehot[r * strips : (r + 1) * strips, :], f_parts[...])
        fill(fea.at[r], found[:, 0:width] + found[:, width : 2 * width])
        one = slice(r, r + 1)
        (to_y if r % 2 else to_zc)(fea.at[one], fea_mid.at[one], 37 + r)
    landed(geo_mid, 4)
    to_y(geo_mid, geo_got, 7)
    for r in range(RANKS):
        one = slice(r, r + 1)
        landed(fea_mid.at[one], 37 + r)
        (to_zc if r % 2 else to_y)(fea_mid.at[one], fea_got.at[one], 41 + r)

    landed(geo_got, 7)

    def turned(x):
        x = jnp.concatenate([x, jnp.zeros((width - strips, width), F32)], axis=0) if strips < width else x
        return jnp.transpose(x)[0 : 8 * RANKS, 0:strips]

    def three(x):
        return jnp.concatenate([part.astype(F32) for part in split3(x)], axis=0).astype(BF16)

    spread = mm(three(turned(rows_of(geo_got, strips))), at_home)
    n8 = 8 * RANKS
    spread = spread[0:n8] + spread[n8 : 2 * n8] + spread[2 * n8 : 3 * n8]
    g = jnp.zeros((8, entries), F32)
    for r in range(RANKS):
        g = g + jnp.where(rank_row == float(r), spread[8 * r : 8 * r + 8, :], 0.0)

    def cam(axis, k):
        return cameras[0, axis, k]

    def center(axis):
        return 8.0 + 4.0 * (
            cam(axis, 0) * g[0:1] + cam(axis, 1) * g[1:2] + cam(axis, 2) * g[2:3] + cam(axis, 3)
        )

    pixel = iota((pixels, 1), 0)
    across = (pixel % 16).astype(F32) + 0.5
    downward = (pixel // 16).astype(F32) + 0.5
    du = across - center(0)
    dv = downward - center(1)
    a = g[3:4] * du
    b = g[4:5] * dv
    skew = g[5:6]
    grown = jnp.exp(-0.5 * (a * a + 2.0 * skew * a * b + b * b))
    solid = 1.0 / (1.0 + jnp.exp(-g[6:7]))
    raw = solid * grown
    alive = jnp.where(iota((1, entries), 1) < lengths[0, 0], 1.0, 0.0)
    cover = jnp.minimum(raw, 0.99) * alive
    fades = jnp.log(1.0 - cover)
    f_high, f_mid, f_low = split3(fades)
    through = jnp.exp(mm(f_high, before) + mm(f_mid, before) + mm(f_low, before))
    weight = cover * through
    weight_high, weight_low = split(weight)

    weight_t_high = jnp.transpose(weight_high.astype(F32)).astype(BF16)
    weight_t_low = jnp.transpose(weight_low.astype(F32)).astype(BF16)
    for r in range(RANKS):
        landed(fea_got.at[r : r + 1], 41 + r)
    high, low = split(rows_of(fea_got, places))
    listed = mm(from_place, jnp.concatenate([high, low], axis=1)).astype(BF16)
    both = mm(weight_high, listed)
    tile = both[:, 0:width] + both[:, width:] + mm(weight_low, listed[:, 0:width])
    image[32 : 32 + pixels, :] = tile

    push(image.at[32:64], image.at[32 + pixels : 64 + pixels], 10, up)
    push(image.at[pixels : 32 + pixels], image.at[0:32], 10, down)
    pending.append((image.at[0:64], 10))

    def sideways(x):
        n = x.shape[0]
        col = iota((n, 1), 0) % 16
        left = jnp.where(col == 0, 0.0, pltpu.roll(x, 1, 0))
        right = jnp.where(col == 15, 0.0, pltpu.roll(x, n - 1, 0))
        return split(jnp.concatenate([left, x, right], axis=1))

    def taps(i):
        return w_parts[i * 3 * width : (i + 1) * 3 * width, :]

    def product(high, low, part):
        both = mm(high, part)
        return both[:, 0:width] + (both[:, width:] + mm(low, part[:, 0:width]))

    edge = jnp.zeros((32, width), F32)
    pic_high, pic_low = sideways(jnp.concatenate([edge, tile, edge], axis=0))
    decoded = jnp.zeros((extended, width), F32)
    for i in range(3):
        here = slice(i * 16, i * 16 + extended)
        decoded = decoded + product(pic_high[here, :], pic_low[here, :], taps(i))
    decoded = decoded + bias[...]
    pic_t_high = jnp.transpose(pic_high.astype(F32)).astype(BF16)
    pic_t_low = jnp.transpose(pic_low.astype(F32)).astype(BF16)
    drain()
    landed(halo_t, 1)
    aim = jnp.concatenate([halo_t[0], targ[...], halo_t[1]], axis=0)
    decoded = decoded - aim

    landed(image.at[0:64], 10)
    has_up = strip > 0
    has_down = strip < strips - 1
    beyond = jnp.concatenate([image[0:32, :], image[32 + pixels :, :]], axis=0)
    known = jnp.where(iota((64, 1), 0) < 32, has_up.astype(F32), has_down.astype(F32)) > 0.5
    out_high, out_low = sideways(jnp.where(known, beyond, 0.0))
    top = product(out_high[0:32, :], out_low[0:32, :], taps(0))
    mid = product(out_high[16:48, :], out_low[16:48, :], taps(1))
    low = product(out_high[32:64, :], out_low[32:64, :], taps(2))
    decoded = jnp.concatenate(
        [
            decoded[0:16] + (top[0:16] + mid[0:16]),
            decoded[16:32] + top[16:32],
            decoded[32 : extended - 32],
            decoded[extended - 32 : extended - 16] + low[0:16],
            decoded[extended - 16 :] + (low[16:32] + mid[16:32]),
        ],
        axis=0,
    )
    rows_at = iota((extended, 1), 0)
    inside = ((rows_at >= 16) | has_up) & ((rows_at < 16 + pixels) | has_down)
    residual = jnp.where(inside, decoded, 0.0)
    res_high, res_low = sideways(residual)
    grad = jnp.zeros((pixels, width), F32)
    for i in range(3):
        here = slice(i * 16, i * 16 + pixels)
        grad = grad + (
            mm(res_high[here, :], w_turned[i, 0], 1, 1)
            + (mm(res_high[here, :], w_turned[i, 1], 1, 1) + mm(res_low[here, :], w_turned[i, 0], 1, 1))
        )
    grad_high, grad_low = split(grad)

    both = mm(weight_t_high, jnp.concatenate([grad_high, grad_low], axis=1))
    f_grad = both[:, 0:width] + (both[:, width:] + mm(weight_t_low, grad_high))
    high, low = split(f_grad)
    f_grad = jnp.concatenate([high, low], axis=1)
    for r in range(RANKS):
        both = mm(to_place[r * strips : (r + 1) * strips, :], f_grad)
        fill(back.at[r], both[:, 0:width] + both[:, width:])
        one = slice(r, r + 1)
        (to_y if r % 2 else to_zc)(back.at[one], back_mid.at[one], 11 + r)

    own = residual[16 : 16 + pixels, :]
    shifted = []
    for i in range(3):
        shifted.append(
            jnp.concatenate(
                [jnp.zeros(((i + 1) * 16, width), F32), own, jnp.zeros((64 - (i + 1) * 16, width), F32)], axis=0
            )
        )
    own_high, own_low = split(jnp.concatenate(shifted, axis=1))
    w_grad = mm(pic_t_high, own_high) + (mm(pic_t_high, own_low) + mm(pic_t_low, own_high))
    next_high = jnp.concatenate([own_high[16:32], own_high[pixels + 32 : pixels + 48]], axis=0)
    next_low = jnp.concatenate([own_low[16:32], own_low[pixels + 32 : pixels + 48]], axis=0)
    near_high, near_low = out_high[16:48], out_low[16:48]
    w_grad = w_grad + (mm(near_high, next_high, 0, 0) + (mm(near_high, next_low, 0, 0) + mm(near_low, next_high, 0, 0)))
    for i in range(3):
        wl[i * 3 * width : (i + 1) * 3 * width, :] = w_grad[:, i * width : (i + 1) * width]
    b_grad = jnp.broadcast_to(jnp.sum(own, axis=0, keepdims=True), (8, width))
    rows_a, rows_b, pa, pb, ra, rb = decoder_rows(sizes)
    core_rows = rows_a + rows_b
    for k in range(nc):
        base = k * core_rows
        wx[k, 0:rows_a, :] = wl[base : base + rows_a, :]
        for i in range(ny):
            at = rows_a + i * (pb + 8)
            wx[k, at : at + pb, :] = wl[base + rows_a + i * pb : base + rows_a + (i + 1) * pb, :]
            wx[k, at + pb : at + pb + 8, :] = b_grad
    other = (v, y, z, 1 - c)
    push(wx.at[1 - c], wc, 15, other)
    pending.append((wc, 15))

    d_weight = mm(jnp.concatenate([grad_high, grad_high], axis=1), listed, 1, 1) + mm(
        grad_low, listed[:, 0:width], 1, 1
    )
    f_high, f_mid, f_low = split3(d_weight * weight)
    later = mm(f_high, behind) + mm(f_mid, behind) + mm(f_low, behind)
    d_cover = d_weight * through - later / (1.0 - cover)
    d_raw = jnp.where(raw < 0.99, d_cover, 0.0) * alive
    d_grown = d_raw * raw
    u = (a + skew * b) * d_grown
    w = (b + skew * a) * d_grown

    def summed(x):
        return jnp.sum(x, axis=0, keepdims=True)

    d_col = 4.0 * g[3:4] * summed(u)
    d_row = 4.0 * g[4:5] * summed(w)
    parts = [cam(0, k) * d_col + cam(1, k) * d_row for k in range(3)]
    parts += [-summed(u * du), -summed(w * dv), -summed(d_grown * a * b), summed(d_grown) * (1.0 - solid)]
    parts.append(jnp.zeros((1, entries), F32))
    g_grad = jnp.concatenate(parts, axis=0)
    by_rank = jnp.concatenate([jnp.where(rank_row == float(r), g_grad, 0.0) for r in range(RANKS)], axis=0)
    by_rank = jnp.concatenate([part.astype(F32) for part in split3(by_rank)] + [jnp.zeros((32, entries), F32)], axis=0)
    fill(bgeo, folded(mm(at_home, by_rank.astype(BF16), 1, 1)))
    to_zc(bgeo, bgeo_mid, 16)

    landed(wc, 15)
    wa[...] = (wx[c, 0:rows_a, :] + wc[0:rows_a, :]).reshape(nz, pa, width)
    wb[...] = (wx[c, rows_a:, :] + wc[rows_a:, :]).reshape(ny, pb + 8, width)

    def along_z(src, dst, n):
        for j in range(1, nz):
            k = (z + j) % nz
            push(src(k), dst(z), n, (v, y, k, c))

    def along_y(src, dst, n):
        for j in range(1, ny):
            k = (y + j) % ny
            push(src(k), dst(y), n, at_y(k))

    def added(ref, n):
        sums = ref[0]
        for k in range(1, n):
            sums = sums + ref[k]
        return sums

    along_z(lambda k: wa.at[k], lambda k: wa_got.at[k], 17)
    keep(wa.at[z], wa_got.at[z], 17)
    along_y(lambda k: wb.at[k], lambda k: wb_got.at[k], 18)
    keep(wb.at[y], wb_got.at[y], 18)
    if nz > 1:
        pending.append((wa.at[0 : nz - 1], 17))
    if ny > 1:
        pending.append((wb.at[0 : ny - 1], 18))

    for r in range(RANKS):
        one = slice(r, r + 1)
        landed(back_mid.at[one], 11 + r)
        (to_zc if r % 2 else to_y)(back_mid.at[one], back_got.at[one], 19 + r)
    landed(bgeo_mid, 16)
    to_y(bgeo_mid, bgeo_got, 23)

    landed(wa_got, 17)
    sums = added(wa_got, nz)
    for k in range(ny):
        fill(wa2.at[k], sums[k * ra : (k + 1) * ra, :])
    along_y(lambda k: wa2.at[k], lambda k: wa2_got.at[k], 24)
    keep(wa2.at[y], wa2_got.at[y], 24)
    landed(wb_got, 18)
    sums = added(wb_got, ny)
    for k in range(nz):
        fill(wb2.at[k, 0:rb], sums[k * rb : (k + 1) * rb, :])
        fill(wb2.at[k, rb : rb + 1], sums[pb : pb + 1, :])
    along_z(lambda k: wb2.at[k], lambda k: wb2_got.at[k], 25)
    keep(wb2.at[z], wb2_got.at[z], 25)
    if ny > 1:
        pending.append((wa2.at[0 : ny - 1], 24))
    if nz > 1:
        pending.append((wb2.at[0 : nz - 1], 25))

    def to_x(src, dst, n):
        for j in range(1, nx):
            push(src, dst, n, at_x((v + j) % nx))

        keep(src, dst, n)
        for _ in range(nx - 1):
            pending.append((src, n))

    def plane(r):
        return all_f.at[v, r]

    drain()
    landed(back_got.at[0:1], 19)
    to_x(back_got.at[0], plane(0), 26)
    landed(bgeo_got, 23)
    to_x(bgeo_got.at[0], all_g.at[v, 0], 30)

    landed(wa2_got, 24)
    landed(wb2_got, 25)
    wq[0:ra] = added(wa2_got, ny)
    wq[ra:] = added(wb2_got, nz)
    to_x(wq, wq_got.at[v], 31)
    for r in range(1, RANKS):
        landed(back_got.at[r : r + 1], 19 + r)
        to_x(back_got.at[r], plane(r), 26 + r)

    if nx > 1:
        landed(asked_all.at[0 : nx - 1], 3)
    slot_at = iota((block, 1), 0).astype(F32).astype(BF16)

    def geometry_of(r):
        return three(jnp.concatenate([shared_g[k][8 * r : 8 * r + 8, :] for k in range(nx)], axis=1))

    def scatter(r):
        asks = jnp.concatenate([asked_all[k][r : r + 1, :] for k in range(nx)], axis=1)
        came_g = geometry_of(r)
        high, low = split(jnp.concatenate([rows_of(all_f.at[k, r], strips) for k in range(nx)], axis=0))
        came = jnp.concatenate([high, low], axis=1)

        @pl.loop(0, prims // rows)
        def _(i):
            here = pl.ds(pl.multiple_of(i * rows, rows), rows)
            base = (i * rows).astype(F32)
            hits = jnp.concatenate(
                [
                    jnp.where(
                        slot_at == (asks - (base + float(k * block))).astype(BF16),
                        jnp.ones((), BF16),
                        jnp.zeros((), BF16),
                    )
                    for k in range(rows // block)
                ],
                axis=0,
            )
            both = mm(hits, came)
            both = both[:, 0:width] + both[:, width:]
            found = mm(came_g, hits, 1, 1)
            found = found[0:8] + found[8:16] + found[16:24]
            if r:
                total[here, :] += both
                total_g[i] += found
            else:
                total[here, :] = both
                total_g[i] = found

    landed(wq_got, 31)
    sums = added(wq_got, nx)
    bias_out[...] = sums[ra + rb]
    wa3[y] = sums[0:ra]
    wb3[z] = sums[ra : ra + rb]
    along_y(lambda k: wa3.at[y], lambda k: wa3.at[k], 32)
    along_z(lambda k: wb3.at[z], lambda k: wb3.at[k], 33)
    if ny > 1:
        pending.append((wa3.at[0 : ny - 1], 32))
    if nz > 1:
        pending.append((wb3.at[0 : nz - 1], 33))

    landed(all_g.at[:, 0], 30)
    shared_g = [turned(rows_of(all_g.at[k], strips)) for k in range(nx)]
    landed(all_f.at[:, 0], 26)
    scatter(0)

    landed(all_f.at[:, 1], 27)
    scatter(1)

    if ny > 1:
        landed(wa3.at[0 : ny - 1], 32)
    if nz > 1:
        landed(wb3.at[0 : nz - 1], 33)

    def part_a(k):
        return wfin.at[c, pl.ds(pl.multiple_of(k * pa, 8), pa)]

    def part_b(k):
        return wfin.at[c, pl.ds(pl.multiple_of(rows_a + k * pb, 8), pb)]

    wfin[c, pl.ds(pl.multiple_of(z * pa, 8), pa), :] = rows_of(wa3, pa)
    wfin[c, pl.ds(pl.multiple_of(rows_a + y * pb, 8), pb), :] = rows_of(wb3, pb)
    along_z(lambda k: part_a(z), part_a, 34)
    along_y(lambda k: part_b(y), part_b, 35)
    gone_a = wfin.at[0, 0 : (nz - 1) * pa]
    gone_b = wfin.at[0, 0 : (ny - 1) * pb]
    if nz > 1:
        pending.append((gone_a, 34))
    if ny > 1:
        pending.append((gone_b, 35))

    landed(all_f.at[:, 2], 28)
    scatter(2)
    landed(all_f.at[:, 3], 29)
    scatter(3)
    save_f = pltpu.make_async_copy(total, feature_out, local.at[3])
    save_f.start()
    for i in range(prims // rows):
        geometry_out[:, i * rows : (i + 1) * rows] = total_g[i][0:7]

    if nz > 1:
        landed(gone_a, 34)
    if ny > 1:
        landed(gone_b, 35)
    push(wfin.at[c], wfin.at[c], 36, other)
    pending.append((wfin.at[0], 36))
    landed(wfin.at[0], 36)
    save_w = pltpu.make_async_copy(wfin, weight_out, local.at[4])
    save_w.start()
    drain()
    save_f.wait()
    save_w.wait()


def decoder_rows(sizes):
    nx, ny, nz, nc, entries, prims, height = sizes
    rows = 9 * 128 // nc
    rows_a = rows * 5 // 9
    rows_b = rows - rows_a
    return rows_a, rows_b, rows_a // nz, rows_b // ny, rows_a // nz // ny, rows_b // nz // ny


def per_device(sizes, *arrays):
    means, inv_scales, correlation, opacity, features, cameras, owners, slots, lengths, target, weights, bias = arrays
    nx, ny, nz, nc, entries, prims, height = sizes
    zc = nz * nc
    strips = ny * zc
    width = 128
    pixels = height * 16
    rows = min(prims, 512)
    rows_a, rows_b, pa, pb, ra, rb = decoder_rows(sizes)
    vmem = pl.BlockSpec(memory_space=pltpu.VMEM)
    smem = pl.BlockSpec(memory_space=pltpu.SMEM)
    any_ = pl.BlockSpec(memory_space=pl.ANY)
    hbm = pl.BlockSpec(memory_space=pltpu.HBM)

    def f32(*shape):
        return pltpu.VMEM(shape, F32)

    def planes(n):
        return f32(n, zc, ny, 1, width)

    geometry, feature, weight, b_grad = pl.pallas_call(
        functools.partial(kernel, sizes),
        name="splat_step",
        out_shape=(
            jax.ShapeDtypeStruct((7, prims), F32),
            jax.ShapeDtypeStruct((prims, width), F32),
            jax.ShapeDtypeStruct((nc, rows_a + rows_b, width), F32),
            jax.ShapeDtypeStruct((1, width), F32),
        ),
        in_specs=[hbm] * 4 + [smem, hbm, hbm, smem, hbm] + [hbm] * 3,
        out_specs=(vmem, any_, any_, vmem),
        scratch_shapes=[
            pltpu.VMEM((1, entries), jnp.int32), pltpu.VMEM((1, entries), jnp.int32), f32(1, width),
            f32(prims, width), f32(pixels, width), f32(9 * width, width), f32(7, prims),
            pltpu.VMEM((width, prims), BF16), pltpu.VMEM((prims, 2 * width), BF16),
            pltpu.VMEM((9 * width, 2 * width), BF16), pltpu.VMEM((3, 2, width, 3 * width), BF16),
            pltpu.VMEM((RANKS * strips, prims), BF16), f32(2, 16, width),
            planes(1), planes(1), planes(1), f32(nx, 8, strips),
            planes(1), planes(1), planes(1), planes(RANKS), planes(RANKS), planes(RANKS),
            f32(pixels + 64, width), planes(RANKS), planes(RANKS), planes(RANKS), planes(1), planes(1), planes(1),
            f32(nx, RANKS, zc, ny, 1, width), f32(nx, 1, zc, ny, 1, width),
            f32(prims, width), f32(prims // rows, 8, rows), f32(9 * width, width),
            f32(nc, rows_a + rows_b + 8 * ny, width), f32(rows_a + rows_b + 8 * ny, width),
            f32(nz, pa, width), f32(nz, pa, width), f32(ny, pb + 8, width), f32(ny, pb + 8, width),
            f32(ny, ra, 1, width), f32(ny, ra, 1, width), f32(nz, rb + 1, 1, width), f32(nz, rb + 1, 1, width),
            f32(ra + rb + 1, 1, width), f32(nx, ra + rb + 1, 1, width),
            f32(ny, ra, 1, width), f32(nz, rb, 1, width), f32(nc, rows_a + rows_b, width),
            pltpu.SemaphoreType.DMA((45,)), pltpu.SemaphoreType.DMA((45,)), pltpu.SemaphoreType.DMA((12,)),
        ],
        compiler_params=pltpu.CompilerParams(
            collective_id=0, has_side_effects=True, vmem_limit_bytes=VMEM_LIMIT
        ),
    )(
        *[a if n == 7 else pltpu.with_memory_space_constraint(a, pltpu.HBM) for n, a in enumerate((
        means, inv_scales, correlation.reshape(1, prims), opacity.reshape(1, prims), cameras,
        owners.reshape(1, entries), slots.reshape(1, entries), lengths.reshape(1, 1), bias.reshape(1, width),
        features, target.reshape(pixels, width), weights.reshape(9 * width, width),
        ))],
    )
    return geometry, feature, weight.reshape(3, 3, width, width), b_grad.reshape(width)


def built(mesh, ny, nz, nc, entries, prims, height):
    nx = mesh.shape["view"]
    finer = Mesh(mesh.devices.reshape(nx, ny, nz, nc), ("view",) + STRIP)
    return jax.shard_map(
        functools.partial(per_device, (nx, ny, nz, nc, entries, prims, height)),
        mesh=finer,
        in_specs=(
            P(None, STRIP),
            P(None, STRIP),
            P(STRIP),
            P(STRIP),
            P(STRIP, None),
            P("view", None, None),
            P("view", STRIP, None, None),
            P("view", STRIP, None),
            P("view", STRIP),
            P("view", STRIP, None, None),
            P(),
            P(),
        ),
        out_specs=(P(None, STRIP), P(STRIP, None), P(), P()),
        check_vma=False,
    )


def solution(mesh):
    return built(mesh, 8, 8, 2, 256, 2048, 16)
```

time: 105 us -> 84.9 us (0.81); the launches traced: 103 us -> 84.7 us
  Pallas kernels: 95.5 us -> 80.5 us
  local copies, waits for them, and re-layouts: 6.39 us -> 2.93 us
    pallas_call x1, Pallas kernels: 95.5 us -> 80.5 us  [per_device(): pl.pallas_call(functools.partial(kernel, sizes), name='splat_step', out_s...]
    unnamed x10 -> x4, local copies, waits for them, and re-layouts: 5.8 us -> 2.93 us
where the time goes in v1:
time: 84.9 us; the launch traced here: 84.7 us
  Pallas kernels  80.5 us (95%)
  local copies, waits for them, and re-layouts  2.93 us (3%)
  between operations  1.29 us (2%)
    pallas_call x1, Pallas kernels, per_device(): pl.pallas_call(functools.partial(kernel, sizes), name='splat_step', out_s...  80.5 us
    unnamed x4, local copies, waits for them, and re-layouts  2.93 us

profile of v1, /device:TPU:1, one launch (start us, length us, event | category | flops | bytes accessed | tf_op | source)
XLA Modules:
  0.0 84.7 jit_solution(822639522895983013)
XLA Ops:
  1.3 80.5 %splat_step.1 = (f32[7,2048]{1,0:T(8,128)S(1)}, f32[2048,128]{1,0:T(8,128)S(1)}, f32[2,576,128]{2,1,0:T(8,128)S(1)}, f32[1,128]{1,0:T(1,128)S(1)}) custom-call(f32[3,2048]{1,0:T(4,128)} %means.1, f32[2,2048]{1,0:T(2,128)} %inv_scales.1, f32[1,2048]{1,0:T(1,128)} %bitcast.13, f32[1,2048]{1,0:T(1,128)} %bitcast.14, f32[1,2,4]{2,1,0:T(2,128)} %cameras.1, ...), custom_call_target="tpu_custom_call" | custom-call | tf_op jit(solution)/shard_map/splat_step/pallas_call | solution.py:667
  81.8 0.6 copy.21
  82.4 1.0 %copy.22 = f32[2048,128]{1,0:T(8,128)} copy(f32[2048,128]{1,0:T(8,128)S(1)} %get-tuple-element.17) | data formatting | bytes 2097152
  83.4 0.8 copy.23
  84.2 0.5 copy.24

commit v2 on v1

--- a/solution.py
+++ b/solution.py
@@ -34,6 +34,10 @@
     rest = x - high.astype(F32)
     mid = rest.astype(BF16)
     return high, mid, (rest - mid.astype(F32)).astype(BF16)
+
+
+def far_first(n):
+    return sorted(range(1, n), key=lambda j: -min(j, n - j))
 
 
 def rows_of(ref, n):
@@ -52,8 +56,8 @@
     owners, slots, bias, feat, targ, wts, table, g_parts, f_parts, w_parts, w_turned, onehot, halo_t,
     req, req_mid, req_got, asked_all,
     geo, geo_mid, geo_got, fea, fea_mid, fea_got,
-    image, back, back_mid, back_got, bgeo, bgeo_mid, bgeo_got, all_f, all_g,
-    total, total_g, wl, wx, wc, wa, wa_got, wb, wb_got, wa2, wa2_got, wb2, wb2_got, wq, wq_got, wa3, wb3, wfin,
+    image, back, back_mid, back_got, bgeo, bgeo_mid, bgeo_got, all_f, all_g, own_g,
+    total, total_g, wl, wx, wc, wa, wa_got, wb, wb_got, wa2, wa2_got, wb2, wb2_got, wq, wq_got, wa3, wb3, mine_a, mine_b, g_total, b_total,
     send, recv, local,
 ):
     nx, ny, nz, nc, entries, prims, height = sizes
@@ -102,13 +106,13 @@
 
     pending = []
 
-    def drain():
-        for ref, n in pending:
+    def drain(count=None):
+        for ref, n in pending[:count]:
             sent(ref, n)
-        pending.clear()
+        del pending[:count]
 
     def to_zc(src, dst, n):
-        for j in range(1, zc_count):
+        for j in far_first(zc_count):
             k = (zc + j) % zc_count
             push(src.at[:, k], dst.at[:, zc], n, at_zc(k))
 
@@ -117,7 +121,7 @@
             pending.append((src.at[:, 0 : zc_count - 1], n))
 
     def to_y(src, dst, n):
-        for j in range(1, ny):
+        for j in far_first(ny):
             k = (y + j) % ny
             push(src.at[:, :, k], dst.at[:, :, y], n, at_y(k))
 
@@ -142,20 +146,17 @@
 
     barrier = pltpu.get_barrier_semaphore()
 
-    for j in range(1, zc_count):
+    for j in far_first(zc_count):
         pl.semaphore_signal(barrier, inc=1, device_id=at_zc((zc + j) % zc_count), device_id_type=MESH)
 
-    for j in range(1, ny):
+    for j in far_first(ny):
         pl.semaphore_signal(barrier, inc=1, device_id=at_y((y + j) % ny), device_id_type=MESH)
 
-    for j in range(1, nx):
+    for j in far_first(nx):
         pl.semaphore_signal(barrier, inc=1, device_id=at_x((v + j) % nx), device_id_type=MESH)
 
     pl.semaphore_signal(barrier, inc=1, device_id=up, device_id_type=MESH)
     pl.semaphore_signal(barrier, inc=1, device_id=down, device_id_type=MESH)
-
-    for load in load_g + [load_f, load_t, load_w, load_b]:
-        load.start()
 
     def column(row):
         n = row.shape[1]
@@ -183,6 +184,8 @@
     pl.semaphore_wait(barrier, zc_count + ny + nx - 3 + 2)
 
     to_zc(req, req_mid, 0)
+    for load in load_g + [load_f, load_w, load_t, load_b]:
+        load.start()
     push(target_hbm.at[0:16], halo_t.at[1], 1, up)
     push(target_hbm.at[pixels - 16 : pixels], halo_t.at[0], 1, down)
     pending.append((halo_t, 1))
@@ -231,7 +234,7 @@
     asked_rows = jnp.transpose(square)[0:8, 0:strips]
     asked_all[v] = asked_rows
 
-    for j in range(1, nx):
+    for j in far_first(nx):
         push(asked_all.at[v], asked_all.at[v], 3, at_x((v + j) % nx))
 
     if nx > 1:
@@ -258,17 +261,18 @@
     fill(geo, folded(packed))
     to_zc(geo, geo_mid, 4)
 
-    for r in range(RANKS):
-        found = mm(onehot[r * strips : (r + 1) * strips, :], f_parts[...])
-        fill(fea.at[r], found[:, 0:width] + found[:, width : 2 * width])
-        one = slice(r, r + 1)
-        (to_y if r % 2 else to_zc)(fea.at[one], fea_mid.at[one], 37 + r)
+    half = RANKS // 2
+    pairs = (slice(0, half), slice(half, RANKS))
+    for n, pair in enumerate(pairs):
+        for r in range(pair.start, pair.stop):
+            found = mm(onehot[r * strips : (r + 1) * strips, :], f_parts[...])
+            fill(fea.at[r], found[:, 0:width] + found[:, width : 2 * width])
+        (to_y if n else to_zc)(fea.at[pair], fea_mid.at[pair], 37 + n)
     landed(geo_mid, 4)
     to_y(geo_mid, geo_got, 7)
-    for r in range(RANKS):
-        one = slice(r, r + 1)
-        landed(fea_mid.at[one], 37 + r)
-        (to_zc if r % 2 else to_y)(fea_mid.at[one], fea_got.at[one], 41 + r)
+    for n, pair in enumerate(pairs):
+        landed(fea_mid.at[pair], 37 + n)
+        (to_zc if n else to_y)(fea_mid.at[pair], fea_got.at[pair], 41 + n)
 
     landed(geo_got, 7)
 
@@ -315,8 +319,8 @@
 
     weight_t_high = jnp.transpose(weight_high.astype(F32)).astype(BF16)
     weight_t_low = jnp.transpose(weight_low.astype(F32)).astype(BF16)
-    for r in range(RANKS):
-        landed(fea_got.at[r : r + 1], 41 + r)
+    for n, pair in enumerate(pairs):
+        landed(fea_got.at[pair], 41 + n)
     high, low = split(rows_of(fea_got, places))
     listed = mm(from_place, jnp.concatenate([high, low], axis=1)).astype(BF16)
     both = mm(weight_high, listed)
@@ -378,25 +382,6 @@
     inside = ((rows_at >= 16) | has_up) & ((rows_at < 16 + pixels) | has_down)
     residual = jnp.where(inside, decoded, 0.0)
     res_high, res_low = sideways(residual)
-    grad = jnp.zeros((pixels, width), F32)
-    for i in range(3):
-        here = slice(i * 16, i * 16 + pixels)
-        grad = grad + (
-            mm(res_high[here, :], w_turned[i, 0], 1, 1)
-            + (mm(res_high[here, :], w_turned[i, 1], 1, 1) + mm(res_low[here, :], w_turned[i, 0], 1, 1))
-        )
-    grad_high, grad_low = split(grad)
-
-    both = mm(weight_t_high, jnp.concatenate([grad_high, grad_low], axis=1))
-    f_grad = both[:, 0:width] + (both[:, width:] + mm(weight_t_low, grad_high))
-    high, low = split(f_grad)
-    f_grad = jnp.concatenate([high, low], axis=1)
-    for r in range(RANKS):
-        both = mm(to_place[r * strips : (r + 1) * strips, :], f_grad)
-        fill(back.at[r], both[:, 0:width] + both[:, width:])
-        one = slice(r, r + 1)
-        (to_y if r % 2 else to_zc)(back.at[one], back_mid.at[one], 11 + r)
-
     own = residual[16 : 16 + pixels, :]
     shifted = []
     for i in range(3):
@@ -427,6 +412,25 @@
     push(wx.at[1 - c], wc, 15, other)
     pending.append((wc, 15))
 
+    grad = jnp.zeros((pixels, width), F32)
+    for i in range(3):
+        here = slice(i * 16, i * 16 + pixels)
+        grad = grad + (
+            mm(res_high[here, :], w_turned[i, 0], 1, 1)
+            + (mm(res_high[here, :], w_turned[i, 1], 1, 1) + mm(res_low[here, :], w_turned[i, 0], 1, 1))
+        )
+    grad_high, grad_low = split(grad)
+
+    both = mm(weight_t_high, jnp.concatenate([grad_high, grad_low], axis=1))
+    f_grad = both[:, 0:width] + (both[:, width:] + mm(weight_t_low, grad_high))
+    high, low = split(f_grad)
+    f_grad = jnp.concatenate([high, low], axis=1)
+    for r in range(RANKS):
+        both = mm(to_place[r * strips : (r + 1) * strips, :], f_grad)
+        fill(back.at[r], both[:, 0:width] + both[:, width:])
+    for n, pair in enumerate(pairs):
+        (to_y if n else to_zc)(back.at[pair], back_mid.at[pair], 11 + n)
+
     d_weight = mm(jnp.concatenate([grad_high, grad_high], axis=1), listed, 1, 1) + mm(
         grad_low, listed[:, 0:width], 1, 1
     )
@@ -457,12 +461,12 @@
     wb[...] = (wx[c, rows_a:, :] + wc[rows_a:, :]).reshape(ny, pb + 8, width)
 
     def along_z(src, dst, n):
-        for j in range(1, nz):
+        for j in far_first(nz):
             k = (z + j) % nz
             push(src(k), dst(z), n, (v, y, k, c))
 
     def along_y(src, dst, n):
-        for j in range(1, ny):
+        for j in far_first(ny):
             k = (y + j) % ny
             push(src(k), dst(y), n, at_y(k))
 
@@ -481,10 +485,9 @@
     if ny > 1:
         pending.append((wb.at[0 : ny - 1], 18))
 
-    for r in range(RANKS):
-        one = slice(r, r + 1)
-        landed(back_mid.at[one], 11 + r)
-        (to_zc if r % 2 else to_y)(back_mid.at[one], back_got.at[one], 19 + r)
+    for n, pair in enumerate(pairs):
+        landed(back_mid.at[pair], 11 + n)
+        (to_zc if n else to_y)(back_mid.at[pair], back_got.at[pair], 19 + n)
     landed(bgeo_mid, 16)
     to_y(bgeo_mid, bgeo_got, 23)
 
@@ -507,7 +510,7 @@
         pending.append((wb2.at[0 : nz - 1], 25))
 
     def to_x(src, dst, n):
-        for j in range(1, nx):
+        for j in far_first(nx):
             push(src, dst, n, at_x((v + j) % nx))
 
         keep(src, dst, n)
@@ -517,11 +520,12 @@
     def plane(r):
         return all_f.at[v, r]
 
-    drain()
-    landed(back_got.at[0:1], 19)
+    older = len(pending)
+    landed(back_got.at[0:half], 19)
     to_x(back_got.at[0], plane(0), 26)
     landed(bgeo_got, 23)
-    to_x(bgeo_got.at[0], all_g.at[v, 0], 30)
+    own_g[...] = turned(rows_of(bgeo_got, strips))
+    to_x(own_g, all_g.at[v], 30)
 
     landed(wa2_got, 24)
     landed(wb2_got, 25)
@@ -529,7 +533,8 @@
     wq[ra:] = added(wb2_got, nz)
     to_x(wq, wq_got.at[v], 31)
     for r in range(1, RANKS):
-        landed(back_got.at[r : r + 1], 19 + r)
+        if r == half:
+            landed(back_got.at[half:RANKS], 20)
         to_x(back_got.at[r], plane(r), 26 + r)
 
     if nx > 1:
@@ -571,9 +576,12 @@
                 total[here, :] = both
                 total_g[i] = found
 
+    drain(older)
     landed(wq_got, 31)
     sums = added(wq_got, nx)
-    bias_out[...] = sums[ra + rb]
+    b_total[...] = sums[ra + rb]
+    save_b = pltpu.make_async_copy(b_total, bias_out, local.at[4])
+    save_b.start()
     wa3[y] = sums[0:ra]
     wb3[z] = sums[ra : ra + rb]
     along_y(lambda k: wa3.at[y], lambda k: wa3.at[k], 32)
@@ -583,8 +591,8 @@
     if nz > 1:
         pending.append((wb3.at[0 : nz - 1], 33))
 
-    landed(all_g.at[:, 0], 30)
-    shared_g = [turned(rows_of(all_g.at[k], strips)) for k in range(nx)]
+    landed(all_g, 30)
+    shared_g = [all_g[k] for k in range(nx)]
     landed(all_f.at[:, 0], 26)
     scatter(0)
 
@@ -597,21 +605,22 @@
         landed(wb3.at[0 : nz - 1], 33)
 
     def part_a(k):
-        return wfin.at[c, pl.ds(pl.multiple_of(k * pa, 8), pa)]
+        return weight_out.at[c, pl.ds(pl.multiple_of(k * pa, 8), pa)]
 
     def part_b(k):
-        return wfin.at[c, pl.ds(pl.multiple_of(rows_a + k * pb, 8), pb)]
-
-    wfin[c, pl.ds(pl.multiple_of(z * pa, 8), pa), :] = rows_of(wa3, pa)
-    wfin[c, pl.ds(pl.multiple_of(rows_a + y * pb, 8), pb), :] = rows_of(wb3, pb)
-    along_z(lambda k: part_a(z), part_a, 34)
-    along_y(lambda k: part_b(y), part_b, 35)
-    gone_a = wfin.at[0, 0 : (nz - 1) * pa]
-    gone_b = wfin.at[0, 0 : (ny - 1) * pb]
-    if nz > 1:
-        pending.append((gone_a, 34))
-    if ny > 1:
-        pending.append((gone_b, 35))
+        return weight_out.at[c, pl.ds(pl.multiple_of(rows_a + k * pb, 8), pb)]
+
+    mine_a[...] = rows_of(wa3, pa)
+    mine_b[...] = rows_of(wb3, pb)
+    along_z(lambda k: mine_a, part_a, 34)
+    along_y(lambda k: mine_b, part_b, 35)
+    keep(mine_a, part_a(z), 34)
+    keep(mine_b, part_b(y), 35)
+    drain()
+    for _ in range(nz - 1):
+        pending.append((mine_a, 34))
+    for _ in range(ny - 1):
+        pending.append((mine_b, 35))
 
     landed(all_f.at[:, 2], 28)
     scatter(2)
@@ -620,20 +629,20 @@
     save_f = pltpu.make_async_copy(total, feature_out, local.at[3])
     save_f.start()
     for i in range(prims // rows):
-        geometry_out[:, i * rows : (i + 1) * rows] = total_g[i][0:7]
-
-    if nz > 1:
-        landed(gone_a, 34)
-    if ny > 1:
-        landed(gone_b, 35)
-    push(wfin.at[c], wfin.at[c], 36, other)
-    pending.append((wfin.at[0], 36))
-    landed(wfin.at[0], 36)
-    save_w = pltpu.make_async_copy(wfin, weight_out, local.at[4])
-    save_w.start()
+        g_total[:, i * rows : (i + 1) * rows] = total_g[i][0:7]
+    save_g = pltpu.make_async_copy(g_total, geometry_out, local.at[2])
+    save_g.start()
+
+    drain()
+    landed(weight_out.at[c, 0:rows_a], 34)
+    landed(weight_out.at[c, rows_a:], 35)
+    push(weight_out.at[c], weight_out.at[c], 36, other)
+    pending.append((weight_out.at[0], 36))
+    landed(weight_out.at[0], 36)
     drain()
     save_f.wait()
-    save_w.wait()
+    save_g.wait()
+    save_b.wait()
 
 
 def decoder_rows(sizes):
@@ -642,6 +651,27 @@
     rows_a = rows * 5 // 9
     rows_b = rows - rows_a
     return rows_a, rows_b, rows_a // nz, rows_b // ny, rows_a // nz // ny, rows_b // nz // ny
+
+
+def passing(count, *refs):
+    moves = [pltpu.make_async_copy(refs[i], refs[count + i], refs[-1].at[i]) for i in range(count)]
+    for move in moves:
+        move.start()
+    for move in moves:
+        move.wait()
+
+
+def hand_over(*arrays):
+    any_ = pl.BlockSpec(memory_space=pl.ANY)
+    return pl.pallas_call(
+        functools.partial(passing, len(arrays)),
+        name="hand_over",
+        out_shape=tuple(jax.ShapeDtypeStruct(a.shape, a.dtype) for a in arrays),
+        in_specs=[any_] * len(arrays),
+        out_specs=(any_,) * len(arrays),
+        scratch_shapes=[pltpu.SemaphoreType.DMA((len(arrays),))],
+        compiler_params=pltpu.CompilerParams(vmem_limit_bytes=1024 * 1024),
+    )(*arrays)
 
 
 def per_device(sizes, *arrays):
@@ -653,7 +683,6 @@
     pixels = height * 16
     rows = min(prims, 512)
     rows_a, rows_b, pa, pb, ra, rb = decoder_rows(sizes)
-    vmem = pl.BlockSpec(memory_space=pltpu.VMEM)
     smem = pl.BlockSpec(memory_space=pltpu.SMEM)
     any_ = pl.BlockSpec(memory_space=pl.ANY)
     hbm = pl.BlockSpec(memory_space=pltpu.HBM)
@@ -674,7 +703,7 @@
             jax.ShapeDtypeStruct((1, width), F32),
         ),
         in_specs=[hbm] * 4 + [smem, hbm, hbm, smem, hbm] + [hbm] * 3,
-        out_specs=(vmem, any_, any_, vmem),
+        out_specs=(any_,) * 4,
         scratch_shapes=[
             pltpu.VMEM((1, entries), jnp.int32), pltpu.VMEM((1, entries), jnp.int32), f32(1, width),
             f32(prims, width), f32(pixels, width), f32(9 * width, width), f32(7, prims),
@@ -684,13 +713,13 @@
             planes(1), planes(1), planes(1), f32(nx, 8, strips),
             planes(1), planes(1), planes(1), planes(RANKS), planes(RANKS), planes(RANKS),
             f32(pixels + 64, width), planes(RANKS), planes(RANKS), planes(RANKS), planes(1), planes(1), planes(1),
-            f32(nx, RANKS, zc, ny, 1, width), f32(nx, 1, zc, ny, 1, width),
+            f32(nx, RANKS, zc, ny, 1, width), f32(nx, 8 * RANKS, strips), f32(8 * RANKS, strips),
             f32(prims, width), f32(prims // rows, 8, rows), f32(9 * width, width),
             f32(nc, rows_a + rows_b + 8 * ny, width), f32(rows_a + rows_b + 8 * ny, width),
             f32(nz, pa, width), f32(nz, pa, width), f32(ny, pb + 8, width), f32(ny, pb + 8, width),
             f32(ny, ra, 1, width), f32(ny, ra, 1, width), f32(nz, rb + 1, 1, width), f32(nz, rb + 1, 1, width),
             f32(ra + rb + 1, 1, width), f32(nx, ra + rb + 1, 1, width),
-            f32(ny, ra, 1, width), f32(nz, rb, 1, width), f32(nc, rows_a + rows_b, width),
+            f32(ny, ra, 1, width), f32(nz, rb, 1, width), f32(pa, width), f32(pb, width), f32(7, prims), f32(1, width),
             pltpu.SemaphoreType.DMA((45,)), pltpu.SemaphoreType.DMA((45,)), pltpu.SemaphoreType.DMA((12,)),
         ],
         compiler_params=pltpu.CompilerParams(
@@ -703,6 +732,7 @@
         features, target.reshape(pixels, width), weights.reshape(9 * width, width),
         ))],
     )
+    geometry, feature, weight, b_grad = hand_over(geometry, feature, weight.reshape(9 * width, width), b_grad)
     return geometry, feature, weight.reshape(3, 3, width, width), b_grad.reshape(width)
 
 

time: 84.9 us -> 78.9 us (0.929)
  Pallas kernels: 80.5 us -> 77.5 us
  local copies, waits for them, and re-layouts: 2.93 us -> 0 us
    pallas_call x1, Pallas kernels: 80.5 us -> 76.2 us  [per_device(): pl.pallas_call(functools.partial(kernel, sizes), name='splat_step', out_s...]
    unnamed x4 -> x0, local copies, waits for them, and re-layouts: 2.93 us -> none
    pallas_call x0 -> x1, Pallas kernels: none -> 1.22 us  [hand_over(): pl.pallas_call(functools.partial(passing, len(arrays)), name='hand_over',...]
where the time goes in v2:
time: 78.9 us; the launch traced here: 78.8 us
  Pallas kernels  77.5 us (98%)
  between operations  1.29 us (2%)
    pallas_call x1, Pallas kernels, per_device(): pl.pallas_call(functools.partial(kernel, sizes), name='splat_step', out_s...  76.2 us

profile of v2, /device:TPU:1, one launch (start us, length us, event | category | flops | bytes accessed | tf_op | source)
XLA Modules:
  0.0 78.8 jit_solution(17669553414298484373)
XLA Ops:
  1.3 76.2 %splat_step.1 = (f32[7,2048]{1,0:T(8,128)S(1)}, f32[2048,128]{1,0:T(8,128)S(1)}, f32[2,576,128]{2,1,0:T(8,128)S(1)}, f32[1,128]{1,0:T(1,128)S(1)}) custom-call(f32[3,2048]{1,0:T(4,128)} %means.1, f32[2,2048]{1,0:T(2,128)} %inv_scales.1, f32[1,2048]{1,0:T(1,128)} %bitcast.13, f32[1,2048]{1,0:T(1,128)} %bitcast.14, f32[1,2,4]{2,1,0:T(2,128)} %cameras.1, ...), custom_call_target="tpu_custom_call" | custom-call | tf_op jit(solution)/shard_map/splat_step/pallas_call | solution.py:696
  77.5 1.2 %hand_over.1 = (f32[7,2048]{1,0:T(8,128)}, f32[2048,128]{1,0:T(8,128)}, f32[1152,128]{1,0:T(8,128)}, f32[1,128]{1,0:T(1,128)}) custom-call(f32[7,2048]{1,0:T(8,128)S(1)} %get-tuple-element.12.refs_0_, f32[2048,128]{1,0:T(8,128)S(1)} %get-tuple-element.13.refs_1_, f32[1152,128]{1,0:T(8,128)S(1)} %bitcast.10, f32[1,128]{1,0:T(1,128)S(1)} %get-tuple-element.15.refs_3_), custom_call_target="tpu_custom_call" | custom-call | tf_op jit(solution)/shard_map/hand_over/pallas_call | solution.py:666

commit v3 on v2

--- a/solution.py
+++ b/solution.py
@@ -50,10 +50,10 @@
 
 def kernel(
     sizes,
-    means, inv_scales, correlation, opacity, cameras, owners_hbm, slots_hbm, lengths, bias_hbm,
+    means, inv_scales, correlation, opacity, cameras_hbm, owners_hbm, slots_hbm, lengths, bias_hbm,
     features_hbm, target_hbm, weights_hbm,
     geometry_out, feature_out, weight_out, bias_out,
-    owners, slots, bias, feat, targ, wts, table, g_parts, f_parts, w_parts, w_turned, onehot, halo_t,
+    owners, slots, bias, cameras, feat, targ, wts, table, g_parts, f_parts, w_parts, w_turned, onehot, halo_t,
     req, req_mid, req_got, asked_all,
     geo, geo_mid, geo_got, fea, fea_mid, fea_got,
     image, back, back_mid, back_got, bgeo, bgeo_mid, bgeo_got, all_f, all_g, own_g,
@@ -132,6 +132,7 @@
     load_o = pltpu.make_async_copy(owners_hbm, owners, local.at[5])
     load_s = pltpu.make_async_copy(slots_hbm, slots, local.at[6])
     load_b = pltpu.make_async_copy(bias_hbm, bias, local.at[7])
+    load_c = pltpu.make_async_copy(cameras_hbm, cameras, local.at[12])
     load_g = [
         pltpu.make_async_copy(ref, table.at[a:b], local.at[8 + i])
         for i, (ref, a, b) in enumerate(
@@ -184,7 +185,7 @@
     pl.semaphore_wait(barrier, zc_count + ny + nx - 3 + 2)
 
     to_zc(req, req_mid, 0)
-    for load in load_g + [load_f, load_w, load_t, load_b]:
+    for load in load_g + [load_f, load_w, load_t, load_b, load_c]:
         load.start()
     push(target_hbm.at[0:16], halo_t.at[1], 1, up)
     push(target_hbm.at[pixels - 16 : pixels], halo_t.at[0], 1, down)
@@ -220,6 +221,7 @@
         w_turned[a, 1, :, b * width : (b + 1) * width] = low
     load_t.wait()
     load_b.wait()
+    load_c.wait()
     rank_col = jnp.sum(jnp.where(alike & (second < first), 1.0, 0.0), axis=1, keepdims=True)
     place_row = rank_row * float(strips) + home
     place_col = rank_col * float(strips) + home_col
@@ -230,16 +232,6 @@
 
     landed(req_got, 2)
     asked = rows_of(req_got, strips)
-    square = jnp.concatenate([asked, jnp.zeros((width - strips, width), F32)], axis=0) if strips < width else asked
-    asked_rows = jnp.transpose(square)[0:8, 0:strips]
-    asked_all[v] = asked_rows
-
-    for j in far_first(nx):
-        push(asked_all.at[v], asked_all.at[v], 3, at_x((v + j) % nx))
-
-    if nx > 1:
-        pending.append((asked_all.at[0 : nx - 1], 3))
-
     block = min(prims, 256)
     ident = iota((1, block), 1).astype(F32).astype(BF16)
     packed = jnp.zeros((strips, width), F32)
@@ -268,6 +260,16 @@
             found = mm(onehot[r * strips : (r + 1) * strips, :], f_parts[...])
             fill(fea.at[r], found[:, 0:width] + found[:, width : 2 * width])
         (to_y if n else to_zc)(fea.at[pair], fea_mid.at[pair], 37 + n)
+    square = jnp.concatenate([asked, jnp.zeros((width - strips, width), F32)], axis=0) if strips < width else asked
+    asked_rows = jnp.transpose(square)[0:8, 0:strips]
+    asked_all[v] = asked_rows
+
+    for j in far_first(nx):
+        push(asked_all.at[v], asked_all.at[v], 3, at_x((v + j) % nx))
+
+    if nx > 1:
+        pending.append((asked_all.at[0 : nx - 1], 3))
+
     landed(geo_mid, 4)
     to_y(geo_mid, geo_got, 7)
     for n, pair in enumerate(pairs):
@@ -291,7 +293,7 @@
         g = g + jnp.where(rank_row == float(r), spread[8 * r : 8 * r + 8, :], 0.0)
 
     def cam(axis, k):
-        return cameras[0, axis, k]
+        return cameras[0, axis : axis + 1, k : k + 1]
 
     def center(axis):
         return 8.0 + 4.0 * (
@@ -409,8 +411,10 @@
             wx[k, at : at + pb, :] = wl[base + rows_a + i * pb : base + rows_a + (i + 1) * pb, :]
             wx[k, at + pb : at + pb + 8, :] = b_grad
     other = (v, y, z, 1 - c)
-    push(wx.at[1 - c], wc, 15, other)
-    pending.append((wc, 15))
+    push(wx.at[1 - c, 0:rows_a], wc.at[0:rows_a], 15, other)
+    push(wx.at[1 - c, rows_a:], wc.at[rows_a:], 45, other)
+    pending.append((wc.at[0:rows_a], 15))
+    pending.append((wc.at[rows_a:], 45))
 
     grad = jnp.zeros((pixels, width), F32)
     for i in range(3):
@@ -430,6 +434,28 @@
         fill(back.at[r], both[:, 0:width] + both[:, width:])
     for n, pair in enumerate(pairs):
         (to_y if n else to_zc)(back.at[pair], back_mid.at[pair], 11 + n)
+
+
+    def along_z(src, dst, n):
+        for j in far_first(nz):
+            k = (z + j) % nz
+            push(src(k), dst(z), n, (v, y, k, c))
+
+    def along_y(src, dst, n):
+        for j in far_first(ny):
+            k = (y + j) % ny
+            push(src(k), dst(y), n, at_y(k))
+
+    def added(ref, n):
+        sums = ref[0]
+        for k in range(1, n):
+            sums = sums + ref[k]
+        return sums
+
+    landed(wc.at[0:rows_a], 15)
+    wa[...] = (wx[c, 0:rows_a, :] + wc[0:rows_a, :]).reshape(nz, pa, width)
+    along_z(lambda k: wa.at[k], lambda k: wa_got.at[k], 17)
+    keep(wa.at[z], wa_got.at[z], 17)
 
     d_weight = mm(jnp.concatenate([grad_high, grad_high], axis=1), listed, 1, 1) + mm(
         grad_low, listed[:, 0:width], 1, 1
@@ -454,32 +480,11 @@
     by_rank = jnp.concatenate([jnp.where(rank_row == float(r), g_grad, 0.0) for r in range(RANKS)], axis=0)
     by_rank = jnp.concatenate([part.astype(F32) for part in split3(by_rank)] + [jnp.zeros((32, entries), F32)], axis=0)
     fill(bgeo, folded(mm(at_home, by_rank.astype(BF16), 1, 1)))
-    to_zc(bgeo, bgeo_mid, 16)
-
-    landed(wc, 15)
-    wa[...] = (wx[c, 0:rows_a, :] + wc[0:rows_a, :]).reshape(nz, pa, width)
+    landed(wc.at[rows_a:], 45)
     wb[...] = (wx[c, rows_a:, :] + wc[rows_a:, :]).reshape(ny, pb + 8, width)
-
-    def along_z(src, dst, n):
-        for j in far_first(nz):
-            k = (z + j) % nz
-            push(src(k), dst(z), n, (v, y, k, c))
-
-    def along_y(src, dst, n):
-        for j in far_first(ny):
-            k = (y + j) % ny
-            push(src(k), dst(y), n, at_y(k))
-
-    def added(ref, n):
-        sums = ref[0]
-        for k in range(1, n):
-            sums = sums + ref[k]
-        return sums
-
-    along_z(lambda k: wa.at[k], lambda k: wa_got.at[k], 17)
-    keep(wa.at[z], wa_got.at[z], 17)
     along_y(lambda k: wb.at[k], lambda k: wb_got.at[k], 18)
     keep(wb.at[y], wb_got.at[y], 18)
+    to_zc(bgeo, bgeo_mid, 16)
     if nz > 1:
         pending.append((wa.at[0 : nz - 1], 17))
     if ny > 1:
@@ -488,8 +493,6 @@
     for n, pair in enumerate(pairs):
         landed(back_mid.at[pair], 11 + n)
         (to_zc if n else to_y)(back_mid.at[pair], back_got.at[pair], 19 + n)
-    landed(bgeo_mid, 16)
-    to_y(bgeo_mid, bgeo_got, 23)
 
     landed(wa_got, 17)
     sums = added(wa_got, nz)
@@ -520,12 +523,11 @@
     def plane(r):
         return all_f.at[v, r]
 
+    landed(bgeo_mid, 16)
+    to_y(bgeo_mid, bgeo_got, 23)
     older = len(pending)
     landed(back_got.at[0:half], 19)
     to_x(back_got.at[0], plane(0), 26)
-    landed(bgeo_got, 23)
-    own_g[...] = turned(rows_of(bgeo_got, strips))
-    to_x(own_g, all_g.at[v], 30)
 
     landed(wa2_got, 24)
     landed(wb2_got, 25)
@@ -536,6 +538,10 @@
         if r == half:
             landed(back_got.at[half:RANKS], 20)
         to_x(back_got.at[r], plane(r), 26 + r)
+        if r == 1:
+            landed(bgeo_got, 23)
+            own_g[...] = turned(rows_of(bgeo_got, strips))
+            to_x(own_g, all_g.at[v], 30)
 
     if nx > 1:
         landed(asked_all.at[0 : nx - 1], 3)
@@ -596,9 +602,6 @@
     landed(all_f.at[:, 0], 26)
     scatter(0)
 
-    landed(all_f.at[:, 1], 27)
-    scatter(1)
-
     if ny > 1:
         landed(wa3.at[0 : ny - 1], 32)
     if nz > 1:
@@ -616,12 +619,13 @@
     along_y(lambda k: mine_b, part_b, 35)
     keep(mine_a, part_a(z), 34)
     keep(mine_b, part_b(y), 35)
-    drain()
     for _ in range(nz - 1):
         pending.append((mine_a, 34))
     for _ in range(ny - 1):
         pending.append((mine_b, 35))
 
+    landed(all_f.at[:, 1], 27)
+    scatter(1)
     landed(all_f.at[:, 2], 28)
     scatter(2)
     landed(all_f.at[:, 3], 29)
@@ -683,7 +687,6 @@
     pixels = height * 16
     rows = min(prims, 512)
     rows_a, rows_b, pa, pb, ra, rb = decoder_rows(sizes)
-    smem = pl.BlockSpec(memory_space=pltpu.SMEM)
     any_ = pl.BlockSpec(memory_space=pl.ANY)
     hbm = pl.BlockSpec(memory_space=pltpu.HBM)
 
@@ -702,10 +705,11 @@
             jax.ShapeDtypeStruct((nc, rows_a + rows_b, width), F32),
             jax.ShapeDtypeStruct((1, width), F32),
         ),
-        in_specs=[hbm] * 4 + [smem, hbm, hbm, smem, hbm] + [hbm] * 3,
+        in_specs=[hbm] * 7 + [pl.BlockSpec(memory_space=pltpu.SMEM)] + [hbm] * 4,
         out_specs=(any_,) * 4,
         scratch_shapes=[
             pltpu.VMEM((1, entries), jnp.int32), pltpu.VMEM((1, entries), jnp.int32), f32(1, width),
+            f32(1, 2, 4),
             f32(prims, width), f32(pixels, width), f32(9 * width, width), f32(7, prims),
             pltpu.VMEM((width, prims), BF16), pltpu.VMEM((prims, 2 * width), BF16),
             pltpu.VMEM((9 * width, 2 * width), BF16), pltpu.VMEM((3, 2, width, 3 * width), BF16),
@@ -720,7 +724,7 @@
             f32(ny, ra, 1, width), f32(ny, ra, 1, width), f32(nz, rb + 1, 1, width), f32(nz, rb + 1, 1, width),
             f32(ra + rb + 1, 1, width), f32(nx, ra + rb + 1, 1, width),
             f32(ny, ra, 1, width), f32(nz, rb, 1, width), f32(pa, width), f32(pb, width), f32(7, prims), f32(1, width),
-            pltpu.SemaphoreType.DMA((45,)), pltpu.SemaphoreType.DMA((45,)), pltpu.SemaphoreType.DMA((12,)),
+            pltpu.SemaphoreType.DMA((46,)), pltpu.SemaphoreType.DMA((46,)), pltpu.SemaphoreType.DMA((13,)),
         ],
         compiler_params=pltpu.CompilerParams(
             collective_id=0, has_side_effects=True, vmem_limit_bytes=VMEM_LIMIT

time: 78.9 us -> 77.3 us (0.980)
  Pallas kernels: 77.5 us -> 75.8 us
    pallas_call x1, Pallas kernels: 76.2 us -> 74.6 us  [per_device(): pl.pallas_call(functools.partial(kernel, sizes), name='splat_step', out_s...]
where the time goes in v3:
time: 77.3 us; the launch traced here: 77.1 us
  Pallas kernels  75.8 us (98%)
  between operations  1.29 us (2%)
    pallas_call x1, Pallas kernels, per_device(): pl.pallas_call(functools.partial(kernel, sizes), name='splat_step', out_s...  74.6 us

profile of v3, /device:TPU:1, one launch (start us, length us, event | category | flops | bytes accessed | tf_op | source)
XLA Modules:
  0.0 77.1 jit_solution(6255678123912746751)
XLA Ops:
  1.3 74.6 %splat_step.1 = (f32[7,2048]{1,0:T(8,128)S(1)}, f32[2048,128]{1,0:T(8,128)S(1)}, f32[2,576,128]{2,1,0:T(8,128)S(1)}, f32[1,128]{1,0:T(1,128)S(1)}) custom-call(f32[3,2048]{1,0:T(4,128)} %means.1, f32[2,2048]{1,0:T(2,128)} %inv_scales.1, f32[1,2048]{1,0:T(1,128)} %bitcast.13, f32[1,2048]{1,0:T(1,128)} %bitcast.14, f32[1,2,4]{2,1,0:T(2,128)} %cameras_hbm.1, ...), custom_call_target="tpu_custom_call" | custom-call | tf_op jit(solution)/shard_map/splat_step/pallas_call | solution.py:699
  75.9 1.2 %hand_over.1 = (f32[7,2048]{1,0:T(8,128)}, f32[2048,128]{1,0:T(8,128)}, f32[1152,128]{1,0:T(8,128)}, f32[1,128]{1,0:T(1,128)}) custom-call(f32[7,2048]{1,0:T(8,128)S(1)} %get-tuple-element.12.refs_0_, f32[2048,128]{1,0:T(8,128)S(1)} %get-tuple-element.13.refs_1_, f32[1152,128]{1,0:T(8,128)S(1)} %bitcast.10, f32[1,128]{1,0:T(1,128)S(1)} %get-tuple-element.15.refs_3_), custom_call_target="tpu_custom_call" | custom-call | tf_op jit(solution)/shard_map/hand_over/pallas_call | solution.py:670

commit v4 on v3

--- a/solution.py
+++ b/solution.py
@@ -550,13 +550,15 @@
     def geometry_of(r):
         return three(jnp.concatenate([shared_g[k][8 * r : 8 * r + 8, :] for k in range(nx)], axis=1))
 
-    def scatter(r):
+    blocks = prims // rows
+
+    def scatter(r, start=0, end=blocks):
         asks = jnp.concatenate([asked_all[k][r : r + 1, :] for k in range(nx)], axis=1)
         came_g = geometry_of(r)
         high, low = split(jnp.concatenate([rows_of(all_f.at[k, r], strips) for k in range(nx)], axis=0))
         came = jnp.concatenate([high, low], axis=1)
 
-        @pl.loop(0, prims // rows)
+        @pl.loop(start, end)
         def _(i):
             here = pl.ds(pl.multiple_of(i * rows, rows), rows)
             base = (i * rows).astype(F32)
@@ -629,7 +631,12 @@
     landed(all_f.at[:, 2], 28)
     scatter(2)
     landed(all_f.at[:, 3], 29)
-    scatter(3)
+    scatter(3, 0, blocks // 2)
+    landed(weight_out.at[c, 0:rows_a], 34)
+    landed(weight_out.at[c, rows_a:], 35)
+    push(weight_out.at[c], weight_out.at[c], 36, other)
+    pending.append((weight_out.at[0], 36))
+    scatter(3, blocks // 2, blocks)
     save_f = pltpu.make_async_copy(total, feature_out, local.at[3])
     save_f.start()
     for i in range(prims // rows):
@@ -638,10 +645,6 @@
     save_g.start()
 
     drain()
-    landed(weight_out.at[c, 0:rows_a], 34)
-    landed(weight_out.at[c, rows_a:], 35)
-    push(weight_out.at[c], weight_out.at[c], 36, other)
-    pending.append((weight_out.at[0], 36))
     landed(weight_out.at[0], 36)
     drain()
     save_f.wait()

time: 77.3 us -> 77.2 us (level)
  no operation moved by 1% of the time
where the time goes in v4:
time: 77.2 us; the launch traced here: 77.1 us
  Pallas kernels  75.8 us (98%)
  between operations  1.29 us (2%)
    pallas_call x1, Pallas kernels, per_device(): pl.pallas_call(functools.partial(kernel, sizes), name='splat_step', out_s...  74.6 us

profile of v4, /device:TPU:1, one launch (start us, length us, event | category | flops | bytes accessed | tf_op | source)
XLA Modules:
  0.0 77.1 jit_solution(8559034824707174617)
XLA Ops:
  1.3 74.6 %splat_step.1 = (f32[7,2048]{1,0:T(8,128)S(1)}, f32[2048,128]{1,0:T(8,128)S(1)}, f32[2,576,128]{2,1,0:T(8,128)S(1)}, f32[1,128]{1,0:T(1,128)S(1)}) custom-call(f32[3,2048]{1,0:T(4,128)} %means.1, f32[2,2048]{1,0:T(2,128)} %inv_scales.1, f32[1,2048]{1,0:T(1,128)} %bitcast.13, f32[1,2048]{1,0:T(1,128)} %bitcast.14, f32[1,2,4]{2,1,0:T(2,128)} %cameras_hbm.1, ...), custom_call_target="tpu_custom_call" | custom-call | tf_op jit(solution)/shard_map/splat_step/pallas_call | solution.py:702
  75.8 1.2 %hand_over.1 = (f32[7,2048]{1,0:T(8,128)}, f32[2048,128]{1,0:T(8,128)}, f32[1152,128]{1,0:T(8,128)}, f32[1,128]{1,0:T(1,128)}) custom-call(f32[7,2048]{1,0:T(8,128)S(1)} %get-tuple-element.12.refs_0_, f32[2048,128]{1,0:T(8,128)S(1)} %get-tuple-element.13.refs_1_, f32[1152,128]{1,0:T(8,128)S(1)} %bitcast.10, f32[1,128]{1,0:T(1,128)S(1)} %get-tuple-element.15.refs_3_), custom_call_target="tpu_custom_call" | custom-call | tf_op jit(solution)/shard_map/hand_over/pallas_call | solution.py:673
